TPU v7x, 32 devices: a whole 2x2x4 slice. The times are simulated.
32 devices in a mesh: dp: 8 (over y, x, core), shard: 4 (over z).
Axes of the slice: x: 2, y: 2, z: 4, core: 2. Of those that a mesh axis runs over, the one named last changes fastest.
Arguments:
- cell_tokens: bfloat16 [32, 1024, 512], P(('dp', 'shard')), may hold values from -6 to 6
- lengths: int32 [32], P(('dp', 'shard')), may hold values from 200 to 1024, as said below
- classes: int32 [32], P(('dp', 'shard')), may hold values 0 or 1
- cotangent: bfloat16 [32, 1024, 512], P(('dp', 'shard')), may hold values from -6 to 6
- weights: float32 [2, 6, 512, 512], P(None, None, 'shard')
- vectors: float32 [2, 9, 512], P(None, None, 'shard')
- first_weights: float32 [2, 6, 512, 512], P(None, None, 'shard'), as said below
- second_weights: float32 [2, 6, 512, 512], P(None, None, 'shard'), as said below
- first_vectors: float32 [2, 9, 512], P(None, None, 'shard'), as said below
- second_vectors: float32 [2, 9, 512], P(None, None, 'shard'), as said below
Outputs:
- activations: bfloat16 [32, 1024, 512], P(('dp', 'shard'))
- input_grad: float32 [32, 1024, 512], P(('dp', 'shard'))
- new_weights: float32 [2, 6, 512, 512], P(None, None, 'shard')
- weights_low: bfloat16 [2, 6, 512, 512], P(None, None, 'shard')
- new_first_weights: float32 [2, 6, 512, 512], P(None, None, 'shard')
- new_second_weights: float32 [2, 6, 512, 512], P(None, None, 'shard')
- new_vectors: float32 [2, 9, 512], P(None, None, 'shard')
- new_first_vectors: float32 [2, 9, 512], P(None, None, 'shard')
- new_second_vectors: float32 [2, 9, 512], P(None, None, 'shard')
- query_bias_grad: float32 [2, 512], P(None, 'shard')
Inputs may be any that keep to these rules, and one draw needn't show every extreme that they name: `lengths`: each cell has 200 to 1024 gene tokens; some cell has exactly 1024. `first_weights`: entries have both signs. `second_weights`: entries are positive. `first_vectors`: entries have both signs. `second_vectors`: entries are positive.
All inputs are finite; a program needn't handle non-finite values. No bound on the sum of `classes` on one device may be relied on, other than what follows from the above.
Results may differ from a plain program's by a relative error of at most 0.022.
Values may be sent and summed in bfloat16 or wider, within the bound.
A program may use at most 256 MiB of HBM per device.

v0:
```python
import math

import jax
import jax.numpy as jnp
from jax import lax
from jax.sharding import PartitionSpec as P

HEADS = 8


beta_first = 0.5
beta_second = 0.55
learn_rate = 0.05
vector_rate = 0.25
decay_rate = 0.01
adam_eps = 1e-08
adam_step = 3.0
norm_eps = 1e-05


def matmul(left, right):
    return jnp.dot(left, right, preferred_element_type=jnp.float32)


def left_transposed(left, right):
    return lax.dot_general(
        left, right, (((0,), (0,)), ((), ())), preferred_element_type=jnp.float32
    )


def right_transposed(left, right):
    return lax.dot_general(
        left, right, (((1,), (1,)), ((), ())), preferred_element_type=jnp.float32
    )


def norm_parts(value, gain, shift):
    center = jnp.mean(value, axis=-1, keepdims=True)
    centered = value - center
    spread = jnp.mean(centered * centered, axis=-1, keepdims=True)
    inverse = lax.rsqrt(spread + norm_eps)
    normed = centered * inverse
    return (normed * gain + shift, normed, inverse)


def norm_backward(grad_in, normed, inverse, gain):
    grad_normed = grad_in * gain
    grad_value = inverse * (
        grad_normed
        - jnp.mean(grad_normed, axis=-1, keepdims=True)
        - normed * jnp.mean(grad_normed * normed, axis=-1, keepdims=True)
    )
    return (grad_value, jnp.sum(grad_in * normed, axis=0), jnp.sum(grad_in, axis=0))


def token_mask(length, klass, row_start, block_rows, token_count):
    row_ids = row_start + jnp.arange(block_rows, dtype=jnp.int32)[:, None]
    col_ids = jnp.arange(token_count, dtype=jnp.int32)[None, :]
    known = (length + 1) // 2
    inside = (row_ids < length) & (col_ids < length) & ((klass == 0) | (col_ids < known))
    return inside | (row_ids == col_ids)


def attend_forward(query, keys, values, lengths, classes):
    token_total, model_width = query.shape
    cell_count = lengths.shape[0]
    token_count = token_total // cell_count
    head_depth = model_width // HEADS
    score_scale = 1.0 / math.sqrt(head_depth)
    block_rows = min(512, token_count)
    outputs = []
    log_sums = []
    key_heads = keys.reshape(token_count, HEADS, head_depth)
    value_heads = values.reshape(token_count, HEADS, head_depth)
    for row_start in range(0, token_count, block_rows):
        query_rows = query[row_start : row_start + block_rows].reshape(
            block_rows, HEADS, head_depth
        )
        scores = (
            jnp.einsum("qhd,khd->hqk", query_rows, key_heads, preferred_element_type=jnp.float32)
            * score_scale
        )
        allowed = token_mask(lengths[0], classes[0], row_start, block_rows, token_count)
        scores = jnp.where(allowed[None], scores, -1e30)
        row_peak = jnp.max(scores, axis=-1, keepdims=True)
        exponent = jnp.exp(scores - row_peak)
        row_total = jnp.sum(exponent, axis=-1, keepdims=True)
        probs_low = (exponent / row_total).astype(jnp.bfloat16)
        mixed = jnp.einsum(
            "hqk,khd->qhd", probs_low, value_heads, preferred_element_type=jnp.float32
        )
        outputs.append(mixed.reshape(block_rows, model_width))
        log_sums.append(row_peak + jnp.log(row_total))
    return (jnp.concatenate(outputs, axis=0), log_sums)


def attend_backward(query, keys, values, grad_mixed, log_sums, lengths, classes):
    token_total, model_width = query.shape
    cell_count = lengths.shape[0]
    token_count = token_total // cell_count
    head_depth = model_width // HEADS
    score_scale = 1.0 / math.sqrt(head_depth)
    block_rows = min(512, token_count)
    grad_query_parts = []
    block_index = 0
    key_heads = keys.reshape(token_count, HEADS, head_depth)
    value_heads = values.reshape(token_count, HEADS, head_depth)
    grad_key_cell = jnp.zeros((token_count, HEADS, head_depth), jnp.float32)
    grad_value_cell = jnp.zeros((token_count, HEADS, head_depth), jnp.float32)
    for row_start in range(0, token_count, block_rows):
        query_rows = query[row_start : row_start + block_rows].reshape(
            block_rows, HEADS, head_depth
        )
        grad_rows = grad_mixed[row_start : row_start + block_rows].reshape(
            block_rows, HEADS, head_depth
        )
        scores = (
            jnp.einsum("qhd,khd->hqk", query_rows, key_heads, preferred_element_type=jnp.float32)
            * score_scale
        )
        allowed = token_mask(lengths[0], classes[0], row_start, block_rows, token_count)
        scores = jnp.where(allowed[None], scores, -1e30)
        probs = jnp.exp(scores - log_sums[block_index])
        block_index = block_index + 1
        probs_low = probs.astype(jnp.bfloat16)
        grad_value_cell = grad_value_cell + jnp.einsum(
            "hqk,qhd->khd", probs_low, grad_rows, preferred_element_type=jnp.float32
        )
        grad_probs = jnp.einsum(
            "qhd,khd->hqk", grad_rows, value_heads, preferred_element_type=jnp.float32
        )
        inner_sum = jnp.sum(probs * grad_probs, axis=-1, keepdims=True)
        grad_scores = (probs * (grad_probs - inner_sum)).astype(jnp.bfloat16)
        grad_query_rows = (
            jnp.einsum("hqk,khd->qhd", grad_scores, key_heads, preferred_element_type=jnp.float32)
            * score_scale
        )
        grad_query_parts.append(grad_query_rows.reshape(block_rows, model_width))
        grad_key_cell = (
            grad_key_cell
            + jnp.einsum(
                "hqk,qhd->khd", grad_scores, query_rows, preferred_element_type=jnp.float32
            )
            * score_scale
        )
    grad_key_parts = grad_key_cell.reshape(token_count, model_width)
    grad_value_parts = grad_value_cell.reshape(token_count, model_width)
    return (jnp.concatenate(grad_query_parts, axis=0), grad_key_parts, grad_value_parts)


def layer_parts(inputs, mats, vecs, lengths, classes):
    inputs_low = inputs.astype(jnp.bfloat16)
    query = (matmul(inputs_low, mats[0]) + vecs[0]).astype(jnp.bfloat16)
    keys = matmul(inputs_low, mats[1]).astype(jnp.bfloat16)
    values = (matmul(inputs_low, mats[2]) + vecs[1]).astype(jnp.bfloat16)
    mixed, log_sums = attend_forward(query, keys, values, lengths, classes)
    mixed_low = mixed.astype(jnp.bfloat16)
    branch = matmul(mixed_low, mats[3]) + vecs[2]
    first_out, first_normed, first_inverse = norm_parts(inputs + branch, vecs[5], vecs[6])
    first_low = first_out.astype(jnp.bfloat16)
    hidden_pre = matmul(first_low, mats[4]) + vecs[3]
    hidden_low = jax.nn.gelu(hidden_pre, approximate=False).astype(jnp.bfloat16)
    feed = matmul(hidden_low, mats[5]) + vecs[4]
    second_out, second_normed, second_inverse = norm_parts(first_out + feed, vecs[7], vecs[8])
    return (
        second_out,
        inputs_low,
        query,
        keys,
        values,
        log_sums,
        mixed_low,
        first_normed,
        first_inverse,
        first_low,
        hidden_pre,
        hidden_low,
        second_normed,
        second_inverse,
    )


def gelu_exact(value):
    return jax.nn.gelu(value, approximate=False)


def layer_backward(inputs, mats, vecs, lengths, classes, grad_out):
    parts = layer_parts(inputs, mats, vecs, lengths, classes)
    inputs_low, query, keys, values, log_sums = (parts[1], parts[2], parts[3], parts[4], parts[5])
    mixed_low, first_normed, first_inverse, first_low = (parts[6], parts[7], parts[8], parts[9])
    hidden_pre, hidden_low, second_normed, second_inverse = (
        parts[10],
        parts[11],
        parts[12],
        parts[13],
    )
    grad_second, grad_gain_two, grad_shift_two = norm_backward(
        grad_out, second_normed, second_inverse, vecs[7]
    )
    grad_feed = grad_second.astype(jnp.bfloat16)
    grad_down = left_transposed(hidden_low, grad_feed)
    grad_bias_down = jnp.sum(grad_feed.astype(jnp.float32), axis=0)
    grad_hidden = right_transposed(grad_feed, mats[5])
    gelu_pull = jax.vjp(gelu_exact, hidden_pre)[1]
    grad_pre = gelu_pull(grad_hidden)[0].astype(jnp.bfloat16)
    grad_up = left_transposed(first_low, grad_pre)
    grad_bias_up = jnp.sum(grad_pre.astype(jnp.float32), axis=0)
    grad_first = grad_second + right_transposed(grad_pre, mats[4])
    grad_sum, grad_gain_one, grad_shift_one = norm_backward(
        grad_first, first_normed, first_inverse, vecs[5]
    )
    grad_branch = grad_sum.astype(jnp.bfloat16)
    grad_proj = left_transposed(mixed_low, grad_branch)
    grad_bias_proj = jnp.sum(grad_branch.astype(jnp.float32), axis=0)
    grad_mixed = right_transposed(grad_branch, mats[3]).astype(jnp.bfloat16)
    grad_query, grad_keys, grad_values = attend_backward(
        query, keys, values, grad_mixed, log_sums, lengths, classes
    )
    grad_query = grad_query.astype(jnp.bfloat16)
    grad_keys = grad_keys.astype(jnp.bfloat16)
    grad_values = grad_values.astype(jnp.bfloat16)
    grad_wq = left_transposed(inputs_low, grad_query)
    grad_wk = left_transposed(inputs_low, grad_keys)
    grad_wv = left_transposed(inputs_low, grad_values)
    grad_bias_query = jnp.sum(grad_query.astype(jnp.float32), axis=0)
    grad_bias_value = jnp.sum(grad_values.astype(jnp.float32), axis=0)
    grad_inputs = (
        grad_sum
        + right_transposed(grad_query, mats[0])
        + right_transposed(grad_keys, mats[1])
        + right_transposed(grad_values, mats[2])
    )
    grad_mats = jnp.stack([grad_wq, grad_wk, grad_wv, grad_proj, grad_up, grad_down])
    grad_vecs = jnp.stack(
        [
            grad_bias_query,
            grad_bias_value,
            grad_bias_proj,
            grad_bias_up,
            grad_bias_down,
            grad_gain_one,
            grad_shift_one,
            grad_gain_two,
            grad_shift_two,
        ]
    )
    return (grad_inputs, grad_mats, grad_vecs)


def adam_update(param, grad, first, second, rate):
    first_new = beta_first * first + (1.0 - beta_first) * grad
    second_new = beta_second * second + (1.0 - beta_second) * grad * grad
    first_hat = first_new / (1.0 - beta_first**adam_step)
    second_hat = second_new / (1.0 - beta_second**adam_step)
    param_new = param - rate * (first_hat / (jnp.sqrt(second_hat) + adam_eps) + decay_rate * param)
    return (param_new, first_new, second_new)


def body(
    cell_tokens,
    lengths,
    classes,
    cotangent,
    weights,
    vectors,
    first_weights,
    second_weights,
    first_vectors,
    second_vectors,
):
    cell_count, token_count, model_width = cell_tokens.shape
    layer_count = weights.shape[0]
    flat_tokens = cell_tokens.reshape(cell_count * token_count, model_width).astype(jnp.float32)
    positions = jnp.arange(token_count, dtype=jnp.int32)[None, :]
    valid = (positions < lengths[:, None]).astype(jnp.float32).reshape(cell_count * token_count, 1)
    stored_inputs = []
    kept_params = []
    current = flat_tokens
    for layer_index in range(layer_count):
        mats, vecs_low = (
            lax.all_gather(weights[layer_index].astype(jnp.bfloat16), "shard", axis=1, tiled=True),
            lax.all_gather(vectors[layer_index].astype(jnp.bfloat16), "shard", axis=1, tiled=True),
        )
        kept_params.append((mats, vecs_low))
        stored_inputs.append(current)
        current = layer_parts(current, mats, vecs_low.astype(jnp.float32), lengths, classes)[0]
    activations = (
        (current * valid).astype(jnp.bfloat16).reshape(cell_count, token_count, model_width)
    )
    grad_current = (
        cotangent.reshape(cell_count * token_count, model_width).astype(jnp.float32) * valid
    )
    grads_mats = [None] * layer_count
    grads_vecs = [None] * layer_count
    for layer_index in reversed(range(layer_count)):
        mats, vecs_low = (
            lax.all_gather(weights[layer_index].astype(jnp.bfloat16), "shard", axis=1, tiled=True),
            lax.all_gather(vectors[layer_index].astype(jnp.bfloat16), "shard", axis=1, tiled=True),
        )
        grad_current, grad_mats, grad_vecs = layer_backward(
            stored_inputs[layer_index],
            mats,
            vecs_low.astype(jnp.float32),
            lengths,
            classes,
            grad_current,
        )
        grads_mats[layer_index] = grad_mats
        grads_vecs[layer_index] = grad_vecs
    stacked_mats = jnp.stack(grads_mats)
    stacked_vecs = jnp.stack(grads_vecs)
    stacked_mats, stacked_vecs = (
        lax.psum_scatter(
            stacked_mats.astype(jnp.bfloat16), "shard", scatter_dimension=2, tiled=True
        ).astype(jnp.float32),
        lax.psum_scatter(
            stacked_vecs.astype(jnp.bfloat16), "shard", scatter_dimension=2, tiled=True
        ).astype(jnp.float32),
    )
    total_mats, total_vecs = (
        lax.psum(stacked_mats.astype(jnp.bfloat16), "dp").astype(jnp.float32),
        lax.psum(stacked_vecs.astype(jnp.bfloat16), "dp").astype(jnp.float32),
    )
    new_weights, new_first_weights, new_second_weights = adam_update(
        weights, total_mats, first_weights, second_weights, learn_rate
    )
    new_vectors, new_first_vectors, new_second_vectors = adam_update(
        vectors, total_vecs, first_vectors, second_vectors, vector_rate
    )
    input_grad = grad_current.reshape(cell_count, token_count, model_width)
    return (
        activations,
        input_grad,
        new_weights,
        new_weights.astype(jnp.bfloat16),
        new_first_weights,
        new_second_weights,
        new_vectors,
        new_first_vectors,
        new_second_vectors,
        total_vecs[:, 0],
    )


def solution(mesh):
    in_specs = (
        P(("dp", "shard"), None, None),
        P(("dp", "shard")),
        P(("dp", "shard")),
        P(("dp", "shard"), None, None),
        P(None, None, "shard", None),
        P(None, None, "shard"),
        P(None, None, "shard", None),
        P(None, None, "shard", None),
        P(None, None, "shard"),
        P(None, None, "shard"),
    )
    out_specs = (
        P(("dp", "shard"), None, None),
        P(("dp", "shard"), None, None),
        P(None, None, "shard", None),
        P(None, None, "shard", None),
        P(None, None, "shard", None),
        P(None, None, "shard", None),
        P(None, None, "shard"),
        P(None, None, "shard"),
        P(None, None, "shard"),
        P(None, "shard"),
    )
    return jax.shard_map(body, mesh=mesh, in_specs=in_specs, out_specs=out_specs, check_vma=False)
```

profile of v0, /device:TPU:0, one launch (start us, length us, event | category | flops | bytes accessed | tf_op | source)
XLA Modules:
  0.0 656.6 jit_solution(9273403954973790990)
XLA Ops:
  12.2 12.9 %all-gather.3 = bf16[1,9,512]{2,0,1:T(2,128)(2,1)S(1)} all-gather(bf16[1,9,128]{2,0,1:T(2,128)(2,1)S(1)} %get-tuple-element.104), channel_id=5, replica_groups=mesh['dp'=8,'shard'=4] {'shard'}, dimensions={2}, use_global_device_ids=true | all-gather | bytes 11520 | tf_op jit(solution)/shard_map/all_gather | solution.py:282
  25.8 8.5 %all-gather.1 = bf16[1,9,512]{2,0,1:T(2,128)(2,1)S(1)} all-gather(bf16[1,9,128]{2,0,1:T(2,128)(2,1)S(1)} %get-tuple-element.105), channel_id=3, replica_groups=mesh['dp'=8,'shard'=4] {'shard'}, dimensions={2}, use_global_device_ids=true | all-gather | bytes 11520 | tf_op jit(solution)/shard_map/all_gather | solution.py:282
  38.8 38.5 %all-gather.7.cloned.1.call-done = bf16[1,6,512,512]{3,2,1,0:T(8,128)(2,1)} async-done(((bf16[1,6,128,512]{3,2,1,0:T(8,128)(2,1)}), bf16[1,6,512,512]{3,2,1,0:T(8,128)(2,1)}) %all-gather.7.cloned.1.call-update) | async-done | bytes 3145744 | tf_op jit(solution)/shard_map/all_gather | solution.py:281
  84.6 3.5 fusion.1
  90.9 3.8 fusion.63
  98.0 4.0 fusion
  103.7 3.8 fusion.64
  108.7 7.1 %multiply_convert_fusion.8 = (bf16[1024,512]{1,0:T(8,128)(2,1)S(1)}, f32[1024,512]{1,0:T(8,128)}, f32[1024,512]{1,0:T(8,128)}) fusion(f32[512]{0:T(512)S(1)} %bitcast.400, bf16[1,6,512,512]{3,2,1,0:T(8,128)(2,1)S(1)} %copy-done.45, f32[1024,512]{0,1:T(8,128)S(1)} %get-tuple-element.113, f32[512]{0:T(512)S(1)} %bitcast.394, f32[512]{0:T(512)S(1)} %bitcast.378, ...), kind=kOutput, calls=%fused_computation.106 | convolution fusion | flops 574095360 | bytes 7878656 | tf_op jit(solution)/shard_map/dot_general | solution.py:22
  119.2 22.3 %all-gather.9.cloned.1.call-done = bf16[1,6,512,512]{3,2,1,0:T(8,128)(2,1)} async-done(((bf16[1,6,128,512]{3,2,1,0:T(8,128)(2,1)}), bf16[1,6,512,512]{3,2,1,0:T(8,128)(2,1)}) %all-gather.9.cloned.1.call-update) | async-done | bytes 3145744 | tf_op jit(solution)/shard_map/all_gather | solution.py:281
  144.9 3.4 fusion.146
  148.3 3.7 fusion.3
  152.9 4.9 fusion.61
  157.8 7.4 %fusion.147 = (f32[8,512]{1,0:T(8,128)S(1)}, f32[8,512,1024]{2,1,0:T(8,128)}) fusion(bf16[512,8,64]{0,2,1:T(8,128)(2,1)S(1)} %bitcast.338, bf16[1024,8,64]{0,2,1:T(8,128)(2,1)S(1)} %bitcast.324, pred[512,1024]{1,0:T(8,128)(4,1)S(1)} %copy-done.36), kind=kOutput, calls=%fused_computation.301 | convolution fusion | flops 549449728 | bytes 18890752 | tf_op jit(solution)/shard_map/qhd,khd->hqk/dot_general | solution.py:80
  165.2 7.7 %fusion.2 = f32[8,512]{1,0:T(8,128)S(1)} fusion(f32[8,512,1024]{2,1,0:T(8,128)} %get-tuple-element.120, f32[8,512]{1,0:T(8,128)S(1)} %get-tuple-element.119), kind=kLoop, calls=%fused_computation.26 | loop fusion | flops 8384512 | bytes 16809984 | tf_op jit(solution)/shard_map/reduce_sum | solution.py:87
  172.9 7.8 %fusion.62 = bf16[8,64,512]{2,1,0:T(8,128)(2,1)S(1)} fusion(bf16[1024,8,64]{0,2,1:T(8,128)(2,1)S(1)} %bitcast.355, f32[8,512,1024]{2,1,0:T(8,128)} %get-tuple-element.120, f32[8,512]{1,0:T(8,128)S(1)} %fusion.2, f32[8,512]{1,0:T(8,128)S(1)} %get-tuple-element.119), kind=kOutput, calls=%fused_computation.167 | convolution fusion | flops 549715968 | bytes 18382848 | tf_op jit(solution)/shard_map/hqk,khd->qhd/dot_general | solution.py:89
  182.5 5.2 multiply_convert_fusion.7
  204.0 4.0 fusion.12
  207.9 10.0 %multiply_reduce_fusion.2 = (f32[8,512]{1,0:T(8,128)}, f32[8,512,1024]{2,1,0:T(8,128)}) fusion(f32[8,512,1024]{2,1,0:T(8,128)S(1)} %get-tuple-element.118, f32[8,512]{1,0:T(8,128)} %copy-done.68, bf16[512,8,64]{0,2,1:T(8,128)(2,1)} %bitcast.347, bf16[1024,8,64]{0,2,1:T(8,128)(2,1)} %bitcast.356), kind=kOutput, calls=%fused_computation.7 | convolution fusion | flops 549449728 | bytes 35160064 | tf_op jit(solution)/shard_map/qhd,khd->hqk/dot_general | solution.py:129
  217.9 12.2 %multiply_reduce_fusion.3 = (f32[8,512]{1,0:T(8,128)}, f32[8,512,1024]{2,1,0:T(8,128)}) fusion(f32[8,512,1024]{2,1,0:T(8,128)} %get-tuple-element.120, f32[8,512]{1,0:T(8,128)S(1)} %log_add_fusion.3, bf16[512,8,64]{0,2,1:T(8,128)(2,1)} %bitcast.342, bf16[1024,8,64]{0,2,1:T(8,128)(2,1)} %bitcast.357), kind=kOutput, calls=%fused_computation.10 | convolution fusion | flops 549449728 | bytes 35160064 | tf_op jit(solution)/shard_map/qhd,khd->hqk/dot_general | solution.py:129
  230.1 11.8 %multiply_convert_fusion.3 = bf16[8,512,1024]{2,1,0:T(8,128)(2,1)S(1)} fusion(f32[8,512,1024]{2,1,0:T(8,128)} %get-tuple-element.128, f32[8,512,1024]{2,1,0:T(8,128)} %get-tuple-element.120, f32[8,512]{1,0:T(8,128)} %get-tuple-element.127, f32[8,512]{1,0:T(8,128)S(1)} %log_add_fusion.3), kind=kLoop, calls=%fused_computation.9 | loop fusion | flops 16777216 | bytes 41975808 | tf_op jit(solution)/shard_map/convert_element_type | solution.py:133
  248.2 7.5 %bitcast_reduce_fusion.5 = (bf16[8,64]{1,0:T(8,128)(2,1)}, bf16[8,64,512]{2,1,0:T(8,128)(2,1)}) fusion(bf16[1024,8,64]{0,2,1:T(8,128)(2,1)S(1)} %bitcast.326, bf16[8,512,1024]{2,1,0:T(8,128)(2,1)} %copy-done.3), kind=kOutput, calls=%fused_computation.224 | convolution fusion | flops 537656832 | bytes 9962496 | tf_op jit(solution)/shard_map/hqk,khd->qhd/dot_general | solution.py:135
  256.3 9.7 %bitcast_reduce_fusion.1 = (bf16[8,64]{1,0:T(8,128)(2,1)}, bf16[8,64,1024]{2,1,0:T(8,128)(2,1)}) fusion(f32[8,64,1024]{2,1,0:T(8,128)} %fusion.12, bf16[512,8,64]{0,2,1:T(8,128)(2,1)S(1)} %bitcast.343, f32[8,512,1024]{2,1,0:T(8,128)} %get-tuple-element.120, f32[8,512]{1,0:T(8,128)S(1)} %log_add_fusion.3), kind=kOutput, calls=%fused_computation.206 | convolution fusion | flops 546831872 | bytes 20464640 | tf_op jit(solution)/shard_map/hqk,qhd->khd/dot_general | solution.py:126
  266.0 10.3 %multiply_convert_fusion.2 = bf16[8,512,1024]{2,1,0:T(8,128)(2,1)} fusion(f32[8,512,1024]{2,1,0:T(8,128)} %get-tuple-element.130, f32[8,512,1024]{2,1,0:T(8,128)S(1)} %get-tuple-element.118, f32[8,512]{1,0:T(8,128)S(1)} %copy-done.73, f32[8,512]{1,0:T(8,128)S(1)} %copy-done.69), kind=kLoop, calls=%fused_computation.6 | loop fusion | flops 16777216 | bytes 41975808 | tf_op jit(solution)/shard_map/convert_element_type | solution.py:133
  276.3 7.2 %bitcast_reduce_fusion.4 = (bf16[8,64]{1,0:T(8,128)(2,1)}, bf16[8,64,512]{2,1,0:T(8,128)(2,1)S(1)}) fusion(bf16[1024,8,64]{0,2,1:T(8,128)(2,1)} %bitcast.325, bf16[8,512,1024]{2,1,0:T(8,128)(2,1)} %multiply_convert_fusion.2), kind=kOutput, calls=%fused_computation.223 | convolution fusion | flops 537656832 | bytes 9962496 | tf_op jit(solution)/shard_map/hqk,khd->qhd/dot_general | solution.py:135
  301.3 9.9 %multiply_reduce_fusion.1 = (f32[8,512]{1,0:T(8,128)}, f32[8,512,1024]{2,1,0:T(8,128)}) fusion(f32[8,512,1024]{2,1,0:T(8,128)S(1)} %bitcast.317, f32[8,512]{1,0:T(8,128)S(1)} %copy-done.67, bf16[512,8,64]{0,2,1:T(8,128)(2,1)S(1)} %bitcast.340, bf16[1024,8,64]{0,2,1:T(8,128)(2,1)} %bitcast.350), kind=kOutput, calls=%fused_computation.4 | convolution fusion | flops 549449728 | bytes 35160064 | tf_op jit(solution)/shard_map/qhd,khd->hqk/dot_general | solution.py:129
  311.2 7.9 %multiply_convert_fusion.1 = bf16[8,512,1024]{2,1,0:T(8,128)(2,1)S(1)} fusion(f32[8,512,1024]{2,1,0:T(8,128)} %get-tuple-element.134, f32[8,512,1024]{2,1,0:T(8,128)S(1)} %bitcast.317, f32[8,512]{1,0:T(8,128)} %get-tuple-element.133, f32[8,512]{1,0:T(8,128)S(1)} %copy-done.67), kind=kLoop, calls=%fused_computation.3 | loop fusion | flops 16777216 | bytes 41975808 | tf_op jit(solution)/shard_map/convert_element_type | solution.py:133
  325.3 7.5 %bitcast_reduce_fusion.3 = (bf16[8,64]{1,0:T(8,128)(2,1)}, bf16[8,64,512]{2,1,0:T(8,128)(2,1)}) fusion(bf16[1024,8,64]{0,2,1:T(8,128)(2,1)S(1)} %bitcast.321, bf16[8,512,1024]{2,1,0:T(8,128)(2,1)} %copy-done.4), kind=kOutput, calls=%fused_computation.222 | convolution fusion | flops 537656832 | bytes 9962496 | tf_op jit(solution)/shard_map/hqk,khd->qhd/dot_general | solution.py:135
  332.8 12.2 %multiply_reduce_fusion = (f32[8,512]{1,0:T(8,128)}, f32[8,512,1024]{2,1,0:T(8,128)}) fusion(f32[8,512,1024]{2,1,0:T(8,128)} %copy-done.1, f32[8,512]{1,0:T(8,128)} %log_add_fusion, bf16[512,8,64]{0,2,1:T(8,128)(2,1)} %bitcast.344, bf16[1024,8,64]{0,2,1:T(8,128)(2,1)} %bitcast.351), kind=kOutput, calls=%fused_computation.1 | convolution fusion | flops 549449728 | bytes 35160064 | tf_op jit(solution)/shard_map/qhd,khd->hqk/dot_general | solution.py:129
  345.0 7.6 %fusion.8 = f32[8,64,1024]{2,1,0:T(8,128)S(1)} fusion(bf16[512,8,64]{0,2,1:T(8,128)(2,1)} %bitcast.345, f32[8,512,1024]{2,1,0:T(8,128)} %copy-done.1, f32[8,512]{1,0:T(8,128)} %log_add_fusion), kind=kOutput, calls=%fused_computation.32 | convolution fusion | flops 545259520 | bytes 19415040 | tf_op jit(solution)/shard_map/hqk,qhd->khd/dot_general | solution.py:126
  354.2 15.3 %multiply_convert_fusion = bf16[8,512,1024]{2,1,0:T(8,128)(2,1)} fusion(f32[8,512,1024]{2,1,0:T(8,128)} %get-tuple-element.136, f32[8,512,1024]{2,1,0:T(8,128)} %copy-done.1, f32[8,512]{1,0:T(8,128)S(1)} %copy-done.74, f32[8,512]{1,0:T(8,128)S(1)} %copy-done.70), kind=kLoop, calls=%fused_computation | loop fusion | flops 16777216 | bytes 41975808 | tf_op jit(solution)/shard_map/convert_element_type | solution.py:133
  369.5 7.6 %bitcast_reduce_fusion.2 = (bf16[8,64]{1,0:T(8,128)(2,1)}, bf16[8,64,512]{2,1,0:T(8,128)(2,1)}) fusion(bf16[1024,8,64]{0,2,1:T(8,128)(2,1)S(1)} %bitcast.322, bf16[8,512,1024]{2,1,0:T(8,128)(2,1)} %multiply_convert_fusion), kind=kOutput, calls=%fused_computation.221 | convolution fusion | flops 537656832 | bytes 9962496 | tf_op jit(solution)/shard_map/hqk,khd->qhd/dot_general | solution.py:135
  377.1 5.0 multiply_convert_fusion.4
  382.1 4.9 bitcast_reduce_fusion
  409.2 14.4 %copy.146 = bf16[2,6,512,512]{3,1,0,2:T(8,128)(2,1)} copy(bf16[2,6,512,512]{2,3,1,0:T(8,128)(2,1)} %pad_maximum_fusion) | data formatting | bytes 12582912
  423.6 13.7 %reshape.518 = bf16[512,6144]{1,0:T(8,128)(2,1)} reshape(bf16[512,2,6,512]{3,2,1,0:T(8,128)(2,1)} %bitcast.318) | data formatting | bytes 12582912
  437.3 3.5 copy.113
  440.9 4.3 copy.111
  445.4 3.5 copy.110
  450.9 3.4 fusion.98
  454.4 92.5 %reduce-scatter.7.cloned.1.call-done = bf16[128,6144]{1,0:T(8,128)(2,1)} async-done(((bf16[512,6144]{1,0:T(8,128)(2,1)}), bf16[128,6144]{1,0:T(8,128)(2,1)}) %reduce-scatter.7.cloned.1.call-update) | async-done | bytes 1572880
  546.9 4.5 reshape.519
  551.3 4.3 copy.147
  561.0 4.9 add_bitcast_fusion
  569.9 14.0 %psum.15 = bf16[2,9,128]{2,1,0:T(8,128)(2,1)S(1)} all-reduce(bf16[2,9,128]{2,1,0:T(8,128)(2,1)S(1)} %copy.149), channel_id=1, replica_groups=mesh['dp'=8,'shard'=4] {'dp'}, use_global_device_ids=true, to_apply=%region_49.50 | all-reduce | flops 2304 | bytes 9216 | tf_op jit(solution)/shard_map/psum | solution.py:322
  586.4 43.3 %all-reduce.2.cloned.1.call-done = bf16[2,6,128,512]{2,3,1,0:T(8,128)(2,1)} async-done(((bf16[2,6,128,512]{2,3,1,0:T(8,128)(2,1)}), bf16[2,6,128,512]{2,3,1,0:T(8,128)(2,1)}) %all-reduce.2.cloned.1.call-update) | async-done | bytes 1572880 | tf_op jit(solution)/shard_map/psum | solution.py:321
  629.7 8.9 %fusion.131 = (bf16[2,6,128,512]{2,3,1,0:T(8,128)(2,1)}, f32[2,6,128,512]{2,3,1,0:T(8,128)}, f32[2,6,128,512]{2,3,1,0:T(8,128)}, f32[2,6,128,512]{2,3,1,0:T(8,128)}) fusion(f32[2,6,128,512]{2,3,1,0:T(8,128)S(1)} %copy-done.19, f32[2,6,128,512]{2,3,1,0:T(8,128)} %copy.111, f32[2,6,128,512]{2,3,1,0:T(8,128)} %copy.110, ...), kind=kLoop, calls=%fused_computation.287 | loop fusion | flops 12582912 | bytes 22020096 | tf_op jit(solution)/shard_map/convert_element_type | solution.py:335
  638.6 3.7 copy.120
  643.8 3.7 copy.122
  (433 shorter events, 122.0 us)
Async XLA Ops:
  7.2 70.1 %all-gather.7.cloned.1.call-start = ((), (), s32[]{:S(2)}) async-start(), calls=%async_computation.3 | async-start | bytes 3932160 | tf_op jit(solution)/shard_map/all_gather | solution.py:281
  9.3 25.6 %copy-start.62 = (bf16[1,1024,512]{2,1,0:T(8,128)(2,1)S(1)}, bf16[1,1024,512]{2,1,0:T(8,128)(2,1)}, u32[]{:S(2)}) copy-start(bf16[1,1024,512]{2,1,0:T(8,128)(2,1)} %param.10) | copy-start | bytes 3145732
  10.7 24.8 %copy-start.61 = (bf16[1,1024,512]{2,1,0:T(8,128)(2,1)S(1)}, bf16[1,1024,512]{2,1,0:T(8,128)(2,1)}, u32[]{:S(2)}) copy-start(bf16[1,1024,512]{2,1,0:T(8,128)(2,1)} %param.13) | copy-start | bytes 3145732
  10.7 130.8 %all-gather.9.cloned.1.call-start = ((), (), s32[]{:S(2)}) async-start(), calls=%async_computation.4 | async-start | bytes 3932160 | tf_op jit(solution)/shard_map/all_gather | solution.py:281
  11.5 535.4 %reduce-scatter.7.cloned.1.call-start = ((), (), s32[]{:S(2)}) async-start(), calls=%async_computation.5 | async-start | bytes 7864320
  34.2 74.5 %copy-start.122 = (f32[1,1,512]{2,0,1:T(1,128)}, f32[1,1,512]{2,0,1:T(1,128)S(1)}, u32[]{:S(2)}) copy-start(f32[1,1,512]{2,0,1:T(1,128)S(1)} %get-tuple-element.95) | copy-start | bytes 6148
  34.2 81.6 %copy-start.89 = (f32[1,1,512]{2,0,1:T(1,128)}, f32[1,1,512]{2,0,1:T(1,128)S(1)}, u32[]{:S(2)}) copy-start(f32[1,1,512]{2,0,1:T(1,128)S(1)} %get-tuple-element.96) | copy-start | bytes 6148
  34.3 81.6 %copy-start.118 = (f32[1,1,512]{2,0,1:T(1,128)}, f32[1,1,512]{2,0,1:T(1,128)S(1)}, u32[]{:S(2)}) copy-start(f32[1,1,512]{2,0,1:T(1,128)S(1)} %get-tuple-element.97) | copy-start | bytes 6148
  34.3 83.6 %copy-start.86 = (f32[1,1,512]{2,0,1:T(1,128)}, f32[1,1,512]{2,0,1:T(1,128)S(1)}, u32[]{:S(2)}) copy-start(f32[1,1,512]{2,0,1:T(1,128)S(1)} %get-tuple-element.92) | copy-start | bytes 6148
  34.3 83.6 %copy-start.100 = (f32[1,1,512]{2,0,1:T(1,128)}, f32[1,1,512]{2,0,1:T(1,128)S(1)}, u32[]{:S(2)}) copy-start(f32[1,1,512]{2,0,1:T(1,128)S(1)} %get-tuple-element.93) | copy-start | bytes 6148
  38.7 42.6 %copy-start.37 = (pred[512,1024]{1,0:T(8,128)(4,1)}, pred[512,1024]{1,0:T(8,128)(4,1)S(1)}, u32[]{:S(2)}) copy-start(pred[512,1024]{1,0:T(8,128)(4,1)S(1)} %get-tuple-element.107) | copy-start | bytes 1572868
  38.8 56.0 %copy-start.35 = (pred[512,1024]{1,0:T(8,128)(4,1)}, pred[512,1024]{1,0:T(8,128)(4,1)S(1)}, u32[]{:S(2)}) copy-start(pred[512,1024]{1,0:T(8,128)(4,1)S(1)} %get-tuple-element.106) | copy-start | bytes 1572868
  79.1 15.6 %copy-start.29 = (bf16[512,512]{0,1:T(8,128)(2,1)}, bf16[512,512]{0,1:T(8,128)(2,1)S(1)}, u32[]{:S(2)}) copy-start(bf16[512,512]{0,1:T(8,128)(2,1)S(1)} %get-tuple-element.81) | copy-start | bytes 1572868
  81.3 13.4 %copy-start.13 = (bf16[1024,512]{0,1:T(8,128)(2,1)}, bf16[1024,512]{0,1:T(8,128)(2,1)S(1)}, u32[]{:S(2)}) copy-start(bf16[1024,512]{0,1:T(8,128)(2,1)S(1)} %convolution_convert_fusion.3) | copy-start | bytes 3145732
  90.3 11.6 %copy-start.39 = (bf16[1024,512]{0,1:T(8,128)(2,1)}, bf16[1024,512]{0,1:T(8,128)(2,1)S(1)}, u32[]{:S(2)}) copy-start(bf16[1024,512]{0,1:T(8,128)(2,1)S(1)} %add_convert_fusion.7) | copy-start | bytes 3145732
  94.7 12.9 %copy-start.132 = (bf16[8,64,512]{2,1,0:T(8,128)(2,1)}, bf16[8,64,512]{2,1,0:T(8,128)(2,1)S(1)}, u32[]{:S(2)}) copy-start(bf16[8,64,512]{2,1,0:T(8,128)(2,1)S(1)} %fusion.63) | copy-start | bytes 1572868
  108.4 7.5 %copy-start.5 = (f32[1024,512]{0,1:T(8,128)}, f32[1024,512]{0,1:T(8,128)S(1)}, u32[]{:S(2)}) copy-start(f32[1024,512]{0,1:T(8,128)S(1)} %get-tuple-element.113) | copy-start | bytes 6291460
  144.1 13.6 %copy-start.31 = (bf16[512,512]{0,1:T(8,128)(2,1)}, bf16[512,512]{0,1:T(8,128)(2,1)S(1)}, u32[]{:S(2)}) copy-start(bf16[512,512]{0,1:T(8,128)(2,1)S(1)} %get-tuple-element.79) | copy-start | bytes 1572868
  144.9 12.8 %copy-start.16 = (bf16[1024,512]{0,1:T(8,128)(2,1)}, bf16[1024,512]{0,1:T(8,128)(2,1)S(1)}, u32[]{:S(2)}) copy-start(bf16[1024,512]{0,1:T(8,128)(2,1)S(1)} %convolution_convert_fusion.2) | copy-start | bytes 3145732
  152.1 51.1 %copy-start.68 = (f32[8,512]{1,0:T(8,128)}, f32[8,512]{1,0:T(8,128)S(1)}, u32[]{:S(2)}) copy-start(f32[8,512]{1,0:T(8,128)S(1)} %log_add_fusion.2) | copy-start | bytes 49156
  152.9 20.0 %copy-start.41 = (bf16[1024,512]{0,1:T(8,128)(2,1)}, bf16[1024,512]{0,1:T(8,128)(2,1)S(1)}, u32[]{:S(2)}) copy-start(bf16[1024,512]{0,1:T(8,128)(2,1)S(1)} %add_convert_fusion.5) | copy-start | bytes 3145732
  172.8 7.8 %copy-start.87 = (f32[1,1,512]{2,0,1:T(1,128)S(1)}, f32[1,1,512]{2,0,1:T(1,128)}, u32[]{:S(2)}) copy-start(f32[1,1,512]{2,0,1:T(1,128)} %copy-done.86) | copy-start | bytes 6148
  172.9 7.8 %copy-start.101 = (f32[1,1,512]{2,0,1:T(1,128)S(1)}, f32[1,1,512]{2,0,1:T(1,128)}, u32[]{:S(2)}) copy-start(f32[1,1,512]{2,0,1:T(1,128)} %copy-done.100) | copy-start | bytes 6148
  172.9 7.8 %copy-start.126 = (f32[1,1,512]{2,0,1:T(1,128)S(1)}, f32[1,1,512]{2,0,1:T(1,128)}, u32[]{:S(2)}) copy-start(f32[1,1,512]{2,0,1:T(1,128)} %get-tuple-element.91) | copy-start | bytes 6148
  172.9 7.8 %copy-start.136 = (bf16[8,64,512]{2,1,0:T(8,128)(2,1)S(1)}, bf16[8,64,512]{2,1,0:T(8,128)(2,1)}, u32[]{:S(2)}) copy-start(bf16[8,64,512]{2,1,0:T(8,128)(2,1)} %fusion.61) | copy-start | bytes 1572868
  181.8 18.4 %copy-start.22 = (f32[1024,512]{0,1:T(8,128)}, f32[1024,512]{0,1:T(8,128)S(1)}, u32[]{:S(2)}) copy-start(f32[1024,512]{0,1:T(8,128)S(1)} %get-tuple-element.122) | copy-start | bytes 6291460
  181.8 18.3 %copy-start.81 = (f32[1024]{0:T(1024)}, f32[1024]{0:T(1024)S(1)}, u32[]{:S(2)}) copy-start(f32[1024]{0:T(1024)S(1)} %broadcast_multiply_fusion.9) | copy-start | bytes 12292
  182.1 18.0 %copy-start.93 = (f32[1024]{0:T(1024)}, f32[1024]{0:T(1024)S(1)}, u32[]{:S(2)}) copy-start(f32[1024]{0:T(1024)S(1)} %add_rsqrt_fusion.1) | copy-start | bytes 12292
  230.1 15.1 %copy-start.32 = (bf16[512,512]{0,1:T(8,128)(2,1)S(1)}, bf16[512,512]{0,1:T(8,128)(2,1)}, u32[]{:S(2)}) copy-start(bf16[512,512]{0,1:T(8,128)(2,1)} %copy-done.31) | copy-start | bytes 1572868
  248.2 7.5 %copy-start.72 = (f32[8,512]{1,0:T(8,128)S(1)}, f32[8,512]{1,0:T(8,128)}, u32[]{:S(2)}) copy-start(f32[8,512]{1,0:T(8,128)} %copy-done.71) | copy-start | bytes 49156
  248.2 7.5 %copy-start.78 = (f32[8,512]{1,0:T(8,128)S(1)}, f32[8,512]{1,0:T(8,128)}, u32[]{:S(2)}) copy-start(f32[8,512]{1,0:T(8,128)} %copy-done.77) | copy-start | bytes 49156
  248.2 8.1 %copy-start.33 = (bf16[512,512]{0,1:T(8,128)(2,1)S(1)}, bf16[512,512]{0,1:T(8,128)(2,1)}, u32[]{:S(2)}) copy-start(bf16[512,512]{0,1:T(8,128)(2,1)} %get-tuple-element.78) | copy-start | bytes 1572868
  256.3 9.7 %copy-start.69 = (f32[8,512]{1,0:T(8,128)S(1)}, f32[8,512]{1,0:T(8,128)}, u32[]{:S(2)}) copy-start(f32[8,512]{1,0:T(8,128)} %copy-done.68) | copy-start | bytes 49156
  256.3 9.7 %copy-start.73 = (f32[8,512]{1,0:T(8,128)S(1)}, f32[8,512]{1,0:T(8,128)}, u32[]{:S(2)}) copy-start(f32[8,512]{1,0:T(8,128)} %get-tuple-element.129) | copy-start | bytes 49156
  311.2 11.2 %copy-start.30 = (bf16[512,512]{0,1:T(8,128)(2,1)S(1)}, bf16[512,512]{0,1:T(8,128)(2,1)}, u32[]{:S(2)}) copy-start(bf16[512,512]{0,1:T(8,128)(2,1)} %copy-done.29) | copy-start | bytes 1572868
  345.0 7.6 %copy-start.50 = (bf16[8,64,512]{2,1,0:T(8,128)(2,1)S(1)}, bf16[8,64,512]{2,1,0:T(8,128)(2,1)}, u32[]{:S(2)}) copy-start(bf16[8,64,512]{2,1,0:T(8,128)(2,1)} %get-tuple-element.138) | copy-start | bytes 1572868
  345.0 7.6 %copy-start.52 = (bf16[8,64,512]{2,1,0:T(8,128)(2,1)S(1)}, bf16[8,64,512]{2,1,0:T(8,128)(2,1)}, u32[]{:S(2)}) copy-start(bf16[8,64,512]{2,1,0:T(8,128)(2,1)} %copy-done.51) | copy-start | bytes 1572868
  345.0 7.6 %copy-start.65 = (bf16[1024,512]{0,1:T(8,128)(2,1)S(1)}, bf16[1024,512]{0,1:T(8,128)(2,1)}, u32[]{:S(2)}) copy-start(bf16[1024,512]{0,1:T(8,128)(2,1)} %fusion.51) | copy-start | bytes 3145732
  354.2 15.3 %copy-start.15 = (bf16[1024,512]{0,1:T(8,128)(2,1)S(1)}, bf16[1024,512]{0,1:T(8,128)(2,1)}, u32[]{:S(2)}) copy-start(bf16[1024,512]{0,1:T(8,128)(2,1)} %copy-done.13) | copy-start | bytes 3145732
  369.5 7.6 %copy-start.18 = (f32[8,64,1024]{2,1,0:T(8,128)S(1)}, f32[8,64,1024]{2,1,0:T(8,128)}, u32[]{:S(2)}) copy-start(f32[8,64,1024]{2,1,0:T(8,128)} %fusion.153) | copy-start | bytes 6291460
  369.5 7.6 %copy-start.27 = (bf16[512,512]{0,1:T(8,128)(2,1)S(1)}, bf16[512,512]{0,1:T(8,128)(2,1)}, u32[]{:S(2)}) copy-start(bf16[512,512]{0,1:T(8,128)(2,1)} %copy-done.26) | copy-start | bytes 1572868
  382.0 16.3 %copy-start.24 = (bf16[8,64,1024]{2,1,0:T(8,128)(2,1)}, bf16[8,64,1024]{2,1,0:T(8,128)(2,1)S(1)}, u32[]{:S(2)}) copy-start(bf16[8,64,1024]{2,1,0:T(8,128)(2,1)S(1)} %multiply_convert_fusion.4) | copy-start | bytes 3145732
  437.3 131.7 %reduce-scatter.9.cloned.1.call-start = ((), (), s32[]{:S(2)}) async-start(), calls=%async_computation.6 | async-start | bytes 163840
  450.7 179.0 %all-reduce.2.cloned.1.call-start = ((), (), s32[]{:S(2)}) async-start(), calls=%async_computation.2 | async-start | bytes 3145728 | tf_op jit(solution)/shard_map/psum | solution.py:321
  565.9 18.6 %copy-start.84 = (f32[2,9,128]{2,0,1:T(2,128)S(1)}, f32[2,9,128]{2,0,1:T(2,128)}, u32[]{:S(2)}) copy-start(f32[2,9,128]{2,0,1:T(2,128)} %param.15) | copy-start | bytes 27652
  565.9 18.6 %copy-start.95 = (f32[2,9,128]{2,0,1:T(2,128)S(1)}, f32[2,9,128]{2,0,1:T(2,128)}, u32[]{:S(2)}) copy-start(f32[2,9,128]{2,0,1:T(2,128)} %param.19) | copy-start | bytes 27652
  565.9 18.6 %copy-start.96 = (f32[2,9,128]{2,0,1:T(2,128)S(1)}, f32[2,9,128]{2,0,1:T(2,128)}, u32[]{:S(2)}) copy-start(f32[2,9,128]{2,0,1:T(2,128)} %param.18) | copy-start | bytes 27652
  565.9 63.8 %copy-start.19 = (f32[2,6,128,512]{2,3,1,0:T(8,128)S(1)}, f32[2,6,128,512]{2,3,1,0:T(8,128)}, u32[]{:S(2)}) copy-start(f32[2,6,128,512]{2,3,1,0:T(8,128)} %copy.113) | copy-start | bytes 9437188
  (107 other events, 312.6 us)
Sparse Core Ops, SparseCore 0:
  10.8 66.3 all-gather.6
  79.4 62.0 all-gather.8
  437.4 109.4 reduce-scatter.6
  549.0 19.9 reduce-scatter.8
  572.6 57.0 all-reduce.1
where the time goes:
time: 667 us; the launch traced here: 657 us
  matrix products  219 us (33%)
  waiting for transfers between devices  197 us (30%)
  local copies, waits for them, and re-layouts  95 us (14%)
  other arithmetic  92.5 us (14%)
  blocking collectives  35.4 us (5%)
  between operations  17 us (3%)
    unnamed x7, waiting for transfers between devices  93.3 us
    unnamed x322, local copies, waits for them, and re-layouts  90 us
    all_gather x2, waiting for transfers between devices, body(): lax.all_gather(weights[layer_index].astype(jnp.bfloat16), 'shard', axis=1...  60.8 us
    convert_element_type x4, other arithmetic, attend_backward(): grad_scores = (probs * (grad_probs - inner_sum)).astype(jnp.bfloat16)  45.4 us
    dot_general x4, matrix products, attend_backward(): jnp.einsum('qhd,khd->hqk', grad_rows, value_heads, preferred_element_type...  44.4 us
    psum x1, waiting for transfers between devices, body(): lax.psum(stacked_mats.astype(jnp.bfloat16), 'dp').astype(jnp.float32)  43.3 us
    dot_general x4, matrix products, attend_backward(): jnp.einsum('hqk,khd->qhd', grad_scores, key_heads, preferred_element_type...  29.7 us
    dot_general x4, matrix products, attend_backward(): jnp.einsum('hqk,qhd->khd', probs_low, grad_rows, preferred_element_type=j...  26.1 us
  transfers between devices with their start and end apart: 5, of which 4 were waited for; matrix products, arithmetic and copies ran while one was open for 13% of the time, Pallas kernels for 0%

commit v1 on v0

v1 whole, which is shorter than its diff:
```python
import functools
import math

import jax
import jax.numpy as jnp
from jax import lax
from jax.experimental import pallas as pl
from jax.experimental.pallas import tpu as pltpu
from jax.sharding import PartitionSpec as P

HEADS = 8
beta_first = 0.5
beta_second = 0.55
learn_rate = 0.05
vector_rate = 0.25
decay_rate = 0.01
adam_eps = 1e-08
adam_step = 3.0
norm_eps = 1e-05

LOG2E = 1.4426950408889634
LN2 = 0.6931471805599453
NEG = -1e30
f32 = jnp.float32
bf16 = jnp.bfloat16
PAIR = 128
RB = 256


def dot(left, right):
    return jnp.dot(left, right, preferred_element_type=f32)


def dot_nt(left, right):
    return lax.dot_general(left, right, (((1,), (1,)), ((), ())), preferred_element_type=f32)


def dot_tn(left, right):
    return lax.dot_general(left, right, (((0,), (0,)), ((), ())), preferred_element_type=f32)


def gelu_parts(value):
    size = jnp.abs(value) * (1.0 / math.sqrt(2.0))
    step = 1.0 / (1.0 + 0.3275911 * size)
    bell = jnp.exp2(value * value * (-0.5 * LOG2E))
    poly = step * (0.254829592 + step * (-0.284496736 + step * (1.421413741 + step * (-1.453152027 + step * 1.061405429))))
    tail = 0.5 * poly * bell
    below = jnp.where(value < 0.0, tail, 1.0 - tail)
    return value * below, below + value * bell * (1.0 / math.sqrt(2.0 * math.pi))


def normalize(value):
    center = jnp.mean(value, axis=-1, keepdims=True)
    centered = value - center
    spread = jnp.mean(centered * centered, axis=-1, keepdims=True)
    inverse = lax.rsqrt(spread + norm_eps)
    return centered * inverse, inverse


def norm_back(grad, normed, inverse, gain):
    scaled = grad * gain
    return inverse * (
        scaled
        - jnp.mean(scaled, axis=-1, keepdims=True)
        - normed * jnp.mean(scaled * normed, axis=-1, keepdims=True)
    )


def lane_masks(rows=1):
    lane = lax.broadcasted_iota(jnp.int32, (rows, PAIR), 1)
    low = jnp.where(lane < 64, 1.0, 0.0)
    return low.astype(bf16), (1.0 - low).astype(bf16)


class Refs:
    pass


def fill_bias(m, known):
    tokens = m.key_bias.shape[0]
    row = lax.broadcasted_iota(jnp.int32, (tokens, PAIR), 0)
    lane = lax.broadcasted_iota(jnp.int32, (tokens, PAIR), 1)
    m.key_bias[...] = jnp.where((lane == 0) & (row >= known), NEG, 0.0).astype(bf16)


def project(m, layer, xb):
    tokens = xb.shape[0]
    scale = LOG2E / 8.0

    def block(index, carry):
        rows = pl.ds(pl.multiple_of(index * 2 * RB, 2 * RB), 2 * RB)
        low = xb[rows, :]
        m.q[layer, rows, :] = ((dot(low, m.w[layer, 0]) + m.vec(layer, 0)) * scale).astype(bf16)
        m.k[layer, rows, :] = dot(low, m.w[layer, 1]).astype(bf16)
        m.v[layer, rows, :] = (dot(low, m.w[layer, 2]) + m.vec(layer, 1)).astype(bf16)
        return carry

    lax.fori_loop(0, tokens // (2 * RB), block, 0)


def probs_copy(m, layer, pair, slot, out):
    here, there = m.probs.at[slot], m.probs_hbm.at[layer, pair]
    if out:
        return pltpu.make_async_copy(here, there, m.probs_sem.at[slot])
    return pltpu.make_async_copy(there, here, m.probs_sem.at[slot])


def attend(m, layer, known):
    tokens, width = m.q.shape[1:]
    pairs = width // PAIR
    masks = lane_masks()
    lane = lax.broadcasted_iota(jnp.int32, (RB, PAIR), 1)
    ones_lane = jnp.where(lane == 0, 1.0, 0.0).astype(bf16)
    eye = lax.broadcasted_iota(jnp.int32, (RB, RB), 0) == lax.broadcasted_iota(jnp.int32, (RB, RB), 1)
    col = lax.broadcasted_iota(jnp.int32, (1, RB), 1)
    blocks = tokens // RB

    def one_pair(pair, carry):
        slot = lax.rem(pair, 2)
        cols = pl.ds(pl.multiple_of(pair * PAIR, PAIR), PAIR)

        @pl.when(pair >= 2)
        def _():
            probs_copy(m, layer, pair - 2, slot, True).wait()

        keys = m.k[layer, :, cols]
        keys_wide = jnp.concatenate([keys, m.key_bias[...]], axis=1)
        values = m.v[layer, :, cols]
        mixed = []
        for head in range(2):
            for block in range(blocks):
                rows = slice(block * RB, (block + 1) * RB)
                query = m.q[layer, rows, cols] * masks[head]
                query_wide = jnp.concatenate([query, ones_lane], axis=1)
                parts = []
                for other in range(blocks):
                    keys_rows = slice(other * RB, (other + 1) * RB)
                    if other == block:
                        part = dot_nt(query, keys[keys_rows])
                        hidden = jnp.where(col + block * RB >= known, NEG, 0.0)
                        part = jnp.where(eye, part, part + hidden)
                    else:
                        part = dot_nt(query_wide, keys_wide[keys_rows])
                    parts.append(part)
                scores = jnp.concatenate(parts, axis=1)
                peak = jnp.max(scores, axis=1, keepdims=True)
                m.probs[slot, head, rows, :] = jnp.exp2(scores - peak).astype(bf16)
            values_wide = values * masks[head] + masks[1 - head]
            mixed.append(dot(m.probs[slot, head], values_wide))
        probs_copy(m, layer, pair, slot, True).start()
        low = lax.broadcasted_iota(jnp.int32, (tokens, PAIR), 1) < 64
        raw = jnp.where(low, mixed[0], mixed[1])
        total = pltpu.roll(jnp.where(low, mixed[1], mixed[0]), 64, 1)
        inverse = 1.0 / total
        m.inv_total[layer, :, cols] = inverse
        m.o[layer, :, cols] = (raw * inverse).astype(bf16)
        return carry

    lax.fori_loop(0, pairs, one_pair, 0)
    for pair in (pairs - 2, pairs - 1):
        probs_copy(m, layer, pair, pair % 2, True).wait()


def feed_forward(m, layer, x_of, y_to):
    tokens = m.q.shape[1]

    def block(index, carry):
        rows = pl.ds(pl.multiple_of(index * RB, RB), RB)
        branch = dot(m.o[layer, rows, :], m.w[layer, 3]) + m.vec(layer, 2)
        normed, inverse = normalize(x_of(rows) + branch)
        m.n1[layer, rows, :] = normed.astype(bf16)
        m.inv1[layer, rows, :] = inverse
        first = normed * m.vec(layer, 5) + m.vec(layer, 6)
        pre = dot(first.astype(bf16), m.w[layer, 4]) + m.vec(layer, 3)
        hidden, slope = gelu_parts(pre)
        low = hidden.astype(bf16)
        m.r[layer, rows, :] = low
        m.slope[layer, rows, :] = slope.astype(bf16)
        feed = dot(low, m.w[layer, 5]) + m.vec(layer, 4)
        normed, inverse = normalize(first + feed)
        m.n2[layer, rows, :] = normed.astype(bf16)
        m.inv2[layer, rows, :] = inverse
        y_to(rows, normed * m.vec(layer, 7) + m.vec(layer, 8))
        return carry

    lax.fori_loop(0, tokens // RB, block, 0)


def column_sum(value):
    rows, width = value.shape
    return jnp.sum(value.reshape(rows // 8, 8, width), axis=0)


def rows_back(m, layer):
    tokens = m.q.shape[1]
    for row in range(8):
        m.sums[row] = jnp.zeros_like(m.sums[row])

    def block(index, carry):
        rows = pl.ds(pl.multiple_of(index * RB, RB), RB)
        grad = m.g[rows, :]
        normed = m.n2[layer, rows, :].astype(f32)
        m.sums[0] += column_sum(grad * normed)
        m.sums[1] += column_sum(grad)
        back = norm_back(grad, normed, m.inv2[layer, rows, :], m.vec(layer, 7))
        m.sums[2] += column_sum(back)
        low = back.astype(bf16)
        m.df[rows, :] = low
        pre = dot_nt(low, m.w[layer, 5]) * m.slope[layer, rows, :].astype(f32)
        m.sums[3] += column_sum(pre)
        low = pre.astype(bf16)
        m.du[rows, :] = low
        grad = back + dot_nt(low, m.w[layer, 4])
        normed = m.n1[layer, rows, :].astype(f32)
        m.sums[4] += column_sum(grad * normed)
        m.sums[5] += column_sum(grad)
        back = norm_back(grad, normed, m.inv1[layer, rows, :], m.vec(layer, 5))
        m.sums[6] += column_sum(back)
        m.g[rows, :] = back
        low = back.astype(bf16)
        m.da[rows, :] = low
        m.do[rows, :] = (dot_nt(low, m.w[layer, 3]) * m.inv_total[layer, rows, :]).astype(bf16)
        first = normed * m.vec(layer, 5) + m.vec(layer, 6)
        m.x1b[rows, :] = first.astype(bf16)
        return carry

    lax.fori_loop(0, tokens // RB, block, 0)
    for row, place in ((0, 7), (1, 8), (2, 4), (3, 3), (4, 5), (5, 6), (6, 2)):
        m.grad_vec(layer, place, jnp.sum(m.sums[row], axis=0, keepdims=True))
    m.grad_mat(layer, 5, dot_tn(m.r[layer], m.df[...]))
    m.grad_mat(layer, 4, dot_tn(m.x1b[...], m.du[...]))
    m.grad_mat(layer, 3, dot_tn(m.o[layer], m.da[...]))


def attend_back(m, layer):
    tokens, width = m.q.shape[1:]
    pairs = width // PAIR
    masks = lane_masks()
    blocks = tokens // RB
    probs_copy(m, layer, 0, 0, False).start()

    def one_pair(pair, carry):
        slot = lax.rem(pair, 2)
        cols = pl.ds(pl.multiple_of(pair * PAIR, PAIR), PAIR)
        probs_copy(m, layer, pair, slot, False).wait()

        @pl.when(pair + 1 < pairs)
        def _():
            probs_copy(m, layer, pair + 1, 1 - slot, False).start()

        grad = m.do[:, cols]
        turned = pltpu.roll(grad.astype(f32) * m.o[layer, :, cols].astype(f32), 64, 1).astype(bf16)
        values = m.v[layer, :, cols]
        keys = m.k[layer, :, cols]
        query_turned = m.q[layer, :, cols].T
        grad_turned = grad.T
        grad_query, grad_keys, grad_values = [], [], []
        for head in range(2):
            part = slice(head * 64, (head + 1) * 64)
            wide = grad * masks[head] - turned * masks[1 - head]
            values_wide = values * masks[head] + masks[1 - head]
            for block in range(blocks):
                rows = slice(block * RB, (block + 1) * RB)
                score = dot_nt(wide[rows], values_wide)
                m.ds[head, rows, :] = score.astype(bf16) * m.probs[slot, head, rows, :]
            grad_values.append(dot(grad_turned[part], m.probs[slot, head]))
            grad_keys.append(dot(query_turned[part], m.ds[head]))
            grad_query.append(dot(m.ds[head], keys))
        low = lax.broadcasted_iota(jnp.int32, (tokens, PAIR), 1) < 64
        m.q[layer, :, cols] = (jnp.where(low, grad_query[0], grad_query[1]) * 0.125).astype(bf16)
        m.k[layer, :, cols] = (jnp.concatenate(grad_keys, axis=0) * LN2).astype(bf16).T
        m.v[layer, :, cols] = jnp.concatenate(grad_values, axis=0).astype(bf16).T
        return carry

    lax.fori_loop(0, pairs, one_pair, 0)


def project_back(m, layer, xb):
    tokens = m.q.shape[1]
    ones = jnp.ones((8, tokens), bf16)
    m.grad_vec(layer, 0, dot(ones, m.q[layer])[0:1])
    m.grad_vec(layer, 1, dot(ones, m.v[layer])[0:1])
    m.grad_mat(layer, 0, dot_tn(xb[...], m.q[layer]))
    m.grad_mat(layer, 1, dot_tn(xb[...], m.k[layer]))
    m.grad_mat(layer, 2, dot_tn(xb[...], m.v[layer]))

    def block(index, carry):
        rows = pl.ds(pl.multiple_of(index * RB, RB), RB)
        m.g[rows, :] = (
            m.g[rows, :]
            + dot_nt(m.q[layer, rows, :], m.w[layer, 0])
            + dot_nt(m.k[layer, rows, :], m.w[layer, 1])
            + dot_nt(m.v[layer, rows, :], m.w[layer, 2])
        )
        return carry

    lax.fori_loop(0, tokens // RB, block, 0)


def kernel(length_ref, class_ref, x_ref, cot_ref, w_ref, vec_ref, act_ref, dx_ref, mats_ref, vecs_ref, probs_hbm,
           q, k, v, o, inv_total, n1, n2, inv1, inv2, r, slope, g, x1, df, du, da, do, x1b, sums, key_bias,
           probs, ds, probs_sem, out_sem):
    m = Refs()
    m.w, m.q, m.k, m.v, m.o, m.inv_total = w_ref, q, k, v, o, inv_total
    m.n1, m.n2, m.inv1, m.inv2, m.r, m.slope, m.g = n1, n2, inv1, inv2, r, slope, g
    m.df, m.du, m.da, m.do, m.x1b, m.sums, m.key_bias = df, du, da, do, x1b, sums, key_bias
    m.probs, m.ds, m.probs_hbm, m.probs_sem = probs, ds, probs_hbm, probs_sem
    m.vec = lambda layer, place: vec_ref[layer, place : place + 1, :]

    def grad_mat(layer, place, value):
        mats_ref[layer, place] = value.astype(bf16)

    def grad_vec(layer, place, value):
        vecs_ref[layer, place : place + 1, :] = value

    m.grad_mat, m.grad_vec = grad_mat, grad_vec
    length, klass = length_ref[0], class_ref[0]
    known = jnp.where(klass == 0, length, (length + 1) // 2)
    tokens = x_ref.shape[0]
    fill_bias(m, known)
    project(m, 0, x_ref)
    attend(m, 0, known)

    def keep_next(rows, value):
        g[rows, :] = value
        x1[rows, :] = value.astype(bf16)

    feed_forward(m, 0, lambda rows: x_ref[rows, :].astype(f32), keep_next)
    project(m, 1, x1)
    attend(m, 1, known)

    def finish(rows, value):
        start = rows.start
        valid = lax.broadcasted_iota(jnp.int32, (RB, 1), 0) + start < length
        act_ref[rows, :] = jnp.where(valid, value, 0.0).astype(bf16)
        g[rows, :] = jnp.where(valid, cot_ref[rows, :].astype(f32), 0.0)

    feed_forward(m, 1, lambda rows: g[rows, :], finish)
    for layer, xb in ((1, x1), (0, x_ref)):
        rows_back(m, layer)
        attend_back(m, layer)
        project_back(m, layer, xb)
    copy = pltpu.make_async_copy(g, dx_ref, out_sem)
    copy.start()
    copy.wait()


def cell_pass(lengths, classes, tokens, cotangent, mats, vecs):
    count, width = tokens.shape
    layers = mats.shape[0]
    pairs = width // PAIR
    vmem = pl.BlockSpec(memory_space=pltpu.VMEM)
    smem = pl.BlockSpec(memory_space=pltpu.SMEM)
    hbm = pl.BlockSpec(memory_space=pl.ANY)
    both = (layers, count, width)
    one = (count, width)
    scratch = [
        pltpu.VMEM(both, bf16), pltpu.VMEM(both, bf16), pltpu.VMEM(both, bf16), pltpu.VMEM(both, bf16),
        pltpu.VMEM(both, f32),
        pltpu.VMEM(both, bf16), pltpu.VMEM(both, bf16),
        pltpu.VMEM((layers, count, 1), f32), pltpu.VMEM((layers, count, 1), f32),
        pltpu.VMEM(both, bf16), pltpu.VMEM(both, bf16),
        pltpu.VMEM(one, f32), pltpu.VMEM(one, bf16),
        pltpu.VMEM(one, bf16), pltpu.VMEM(one, bf16), pltpu.VMEM(one, bf16), pltpu.VMEM(one, bf16), pltpu.VMEM(one, bf16),
        pltpu.VMEM((8, 8, width), f32),
        pltpu.VMEM((count, PAIR), bf16),
        pltpu.VMEM((2, 2, count, count), bf16),
        pltpu.VMEM((2, count, count), bf16),
        pltpu.SemaphoreType.DMA((2,)),
        pltpu.SemaphoreType.DMA,
    ]
    outs = pl.pallas_call(
        kernel,
        out_shape=[
            jax.ShapeDtypeStruct(one, bf16),
            jax.ShapeDtypeStruct(one, f32),
            jax.ShapeDtypeStruct(mats.shape, bf16),
            jax.ShapeDtypeStruct((layers, 16, width), f32),
            jax.ShapeDtypeStruct((layers, pairs, 2, count, count), bf16),
        ],
        in_specs=[smem, smem, vmem, vmem, vmem, vmem],
        out_specs=[vmem, hbm, vmem, vmem, hbm],
        scratch_shapes=scratch,
        compiler_params=pltpu.CompilerParams(vmem_limit_bytes=67043328),
    )(lengths, classes, tokens, cotangent, mats, vecs)
    return outs[:4]


def adam_update(param, grad, first, second, rate):
    first_new = beta_first * first + (1.0 - beta_first) * grad
    second_new = beta_second * second + (1.0 - beta_second) * grad * grad
    first_hat = first_new / (1.0 - beta_first**adam_step)
    second_hat = second_new / (1.0 - beta_second**adam_step)
    param_new = param - rate * (first_hat / (jnp.sqrt(second_hat) + adam_eps) + decay_rate * param)
    return (param_new, first_new, second_new)


def body(
    cell_tokens,
    lengths,
    classes,
    cotangent,
    weights,
    vectors,
    first_weights,
    second_weights,
    first_vectors,
    second_vectors,
):
    cell_count, token_count, model_width = cell_tokens.shape
    mats = lax.all_gather(weights.astype(bf16), "shard", axis=2, tiled=True)
    vecs = lax.all_gather(vectors.astype(bf16), "shard", axis=2, tiled=True).astype(f32)
    vecs = jnp.pad(vecs, ((0, 0), (0, 16 - vecs.shape[1]), (0, 0)))
    activations, input_grad, grad_mats, grad_vecs = cell_pass(
        lengths, classes, cell_tokens[0], cotangent[0], mats, vecs
    )
    grad_vecs = grad_vecs[:, : vectors.shape[1]]
    total_mats = lax.psum_scatter(grad_mats, "shard", scatter_dimension=2, tiled=True)
    total_vecs = lax.psum_scatter(grad_vecs.astype(bf16), "shard", scatter_dimension=2, tiled=True)
    total_mats = lax.psum(total_mats, "dp").astype(f32)
    total_vecs = lax.psum(total_vecs, "dp").astype(f32)
    new_weights, new_first_weights, new_second_weights = adam_update(
        weights, total_mats, first_weights, second_weights, learn_rate
    )
    new_vectors, new_first_vectors, new_second_vectors = adam_update(
        vectors, total_vecs, first_vectors, second_vectors, vector_rate
    )
    return (
        activations[None],
        input_grad[None],
        new_weights,
        new_weights.astype(bf16),
        new_first_weights,
        new_second_weights,
        new_vectors,
        new_first_vectors,
        new_second_vectors,
        total_vecs[:, 0],
    )


def solution(mesh):
    in_specs = (
        P(("dp", "shard"), None, None),
        P(("dp", "shard")),
        P(("dp", "shard")),
        P(("dp", "shard"), None, None),
        P(None, None, "shard", None),
        P(None, None, "shard"),
        P(None, None, "shard", None),
        P(None, None, "shard", None),
        P(None, None, "shard"),
        P(None, None, "shard"),
    )
    out_specs = (
        P(("dp", "shard"), None, None),
        P(("dp", "shard"), None, None),
        P(None, None, "shard", None),
        P(None, None, "shard", None),
        P(None, None, "shard", None),
        P(None, None, "shard", None),
        P(None, None, "shard"),
        P(None, None, "shard"),
        P(None, None, "shard"),
        P(None, "shard"),
    )
    return jax.shard_map(body, mesh=mesh, in_specs=in_specs, out_specs=out_specs, check_vma=False)
```

time: 667 us -> 447 us (0.67); the launches traced: 657 us -> 447 us
  matrix products: 219 us -> 0 us
  Pallas kernels: 0 us -> 111 us
  local copies, waits for them, and re-layouts: 95 us -> 5.06 us
  waiting for transfers between devices: 197 us -> 277 us
  other arithmetic: 92.5 us -> 12.9 us
  blocking collectives: 35.4 us -> 26.1 us
    dot_general x60 -> x0, matrix products: 219 us -> none  [the longest x4 44.4 us: attend_backward(): jnp.einsum('qhd,khd->hqk', grad_rows, value_heads, preferred_element_type...]
    pallas_call x0 -> x1, Pallas kernels: none -> 111 us  [cell_pass(): pl.pallas_call(kernel, out_shape=[jax.ShapeDtypeStruct(one, bf16), jax.Sh...]
    reduce_scatter x0 -> x1, waiting for transfers between devices: none -> 107 us  [body(): lax.psum_scatter(grad_mats, 'shard', scatter_dimension=2, tiled=True)]
    unnamed x322 -> x19, local copies, waits for them, and re-layouts: 90 us -> 4.49 us
    unnamed x7 -> x5, waiting for transfers between devices: 93.3 us -> 22.8 us
    convert_element_type x7 -> x3, other arithmetic: 56.2 us -> 12.2 us  [the longest x1 8.95 us: body(): new_weights.astype(bf16)]
    all_gather x2 -> x1, waiting for transfers between devices: 60.8 us -> 103 us  [body(): mats = lax.all_gather(weights.astype(bf16), 'shard', axis=2, tiled=True)]
    reduce_sum x15 -> x0, other arithmetic: 28.3 us -> none  [the longest x4 18.9 us: attend_forward(): row_total = jnp.sum(exponent, axis=-1, keepdims=True)]
  transfers between devices with their start and end apart: 5 -> 4, of which waited for: 4 -> 4; matrix products, arithmetic and copies ran while one was open for 13% -> 1% of each run, Pallas kernels for 0% -> 0%
where the time goes in v1:
time: 447 us
  waiting for transfers between devices  277 us (62%)
  Pallas kernels  111 us (25%)
  blocking collectives  26.1 us (6%)
  between operations  15.2 us (3%)
  other arithmetic  12.9 us (3%)
  local copies, waits for them, and re-layouts  5.06 us (1%)
    pallas_call x1, Pallas kernels, cell_pass(): pl.pallas_call(kernel, out_shape=[jax.ShapeDtypeStruct(one, bf16), jax.Sh...  111 us
    reduce_scatter x1, waiting for transfers between devices, body(): lax.psum_scatter(grad_mats, 'shard', scatter_dimension=2, tiled=True)  107 us
    all_gather x1, waiting for transfers between devices, body(): mats = lax.all_gather(weights.astype(bf16), 'shard', axis=2, tiled=True)  103 us
    psum x1, waiting for transfers between devices, body(): total_mats = lax.psum(total_mats, 'dp').astype(f32)  44.3 us
    unnamed x5, waiting for transfers between devices  22.8 us
    all_gather x1, blocking collectives, body(): lax.all_gather(vectors.astype(bf16), 'shard', axis=2, tiled=True)  13.6 us
    psum x1, blocking collectives, body(): total_vecs = lax.psum(total_vecs, 'dp').astype(f32)  12.4 us
    convert_element_type x1, other arithmetic, body(): new_weights.astype(bf16)  8.95 us
  transfers between devices with their start and end apart: 4, of which 4 were waited for; matrix products, arithmetic and copies ran while one was open for 1% of the time, Pallas kernels for 0%

profile of v1, /device:TPU:0, one launch (start us, length us, event | category | flops | bytes accessed | tf_op | source)
XLA Modules:
  0.0 447.0 jit_solution(11752526682170447270)
XLA Ops:
  7.2 0.0 copy-start.1
  7.2 0.0 all-gather.2.cloned.1.call-start
  7.2 3.2 convert_element_type.19
  10.5 0.0 all-gather.2.cloned.1.call-update
  10.5 0.0 reduce-scatter.5.cloned.1.call-start
  11.9 0.0 copy-done.1
  11.9 13.6 %all_gather.7 = bf16[2,9,512]{2,1,0:T(8,128)(2,1)S(1)} all-gather(bf16[2,9,128]{2,1,0:T(8,128)(2,1)S(1)} %copy.36), channel_id=1, replica_groups=mesh['dp'=8,'shard'=4] {'shard'}, dimensions={2}, use_global_device_ids=true | all-gather | bytes 23040 | tf_op jit(solution)/shard_map/all_gather | solution.py:412
  25.5 0.6 pad_convert_fusion.vec_ref
  26.2 102.5 %all-gather.2.cloned.1.call-done.w_ref = bf16[2,6,512,512]{3,2,1,0:T(8,128)(2,1)} async-done(((bf16[2,6,128,512]{3,2,1,0:T(8,128)(2,1)}), bf16[2,6,512,512]{3,2,1,0:T(8,128)(2,1)}) %all-gather.2.cloned.1.call-update) | async-done | bytes 6291472 | tf_op jit(solution)/shard_map/all_gather | solution.py:411
  128.7 110.7 %shard_map.177 = (bf16[1024,512]{1,0:T(8,128)(2,1)}, f32[1024,512]{1,0:T(8,128)}, bf16[2,6,512,512]{3,2,1,0:T(8,128)(2,1)}, f32[2,16,512]{2,1,0:T(8,128)}, bf16[2,4,2,1024,1024]{4,3,2,1,0:T(8,128)(2,1)}) custom-call(s32[1]{0:T(128)S(6)} %copy.65.length_ref, s32[1]{0:T(128)S(6)} %copy.66.class_ref, bf16[1024,512]{1,0:T(8,128)(2,1)} %bitcast.7, ...), custom_call_target="tpu_custom_call" | custom-call | tf_op jit(solution)/shard_map/pallas_call | solution.py:372
  239.4 0.0 copy-start.3
  239.5 0.0 copy-start.2
  239.5 0.0 copy-start.4
  239.5 0.0 copy-start.5
  239.5 0.0 copy-start
  239.5 0.0 reduce-scatter.5.cloned.1.call-update
  239.5 0.0 reduce-scatter.7.cloned.1.call-start
  239.6 0.7 copy-done.3
  240.3 0.2 copy.44
  240.5 0.8 reshape.20
  241.3 0.0 reduce-scatter.7.cloned.1.call-update
  241.3 0.0 all-reduce.3.cloned.1.call-start
  241.4 107.3 %reduce-scatter.5.cloned.1.call-done = bf16[2,6,128,512]{3,2,1,0:T(8,128)(2,1)} async-done(((bf16[2,6,512,512]{3,2,1,0:T(8,128)(2,1)}), bf16[2,6,128,512]{3,2,1,0:T(8,128)(2,1)}) %reduce-scatter.5.cloned.1.call-update) | async-done | bytes 1572880 | tf_op jit(solution)/shard_map/reduce_scatter | solution.py:418
  348.6 0.0 all-reduce.3.cloned.1.call-update
  348.7 22.8 %reduce-scatter.7.cloned.1.call-done = bf16[128,18]{1,0:T(8,128)(2,1)} async-done(((bf16[512,18]{1,0:T(8,128)(2,1)}), bf16[128,18]{1,0:T(8,128)(2,1)}) %reduce-scatter.7.cloned.1.call-update) | async-done | bytes 4624
  371.5 0.8 reshape.21
  372.3 0.1 copy.45
  372.4 12.4 %psum.15 = bf16[2,9,128]{2,1,0:T(8,128)(2,1)S(1)} all-reduce(bf16[2,9,128]{2,1,0:T(8,128)(2,1)S(1)} %copy.45), channel_id=1, replica_groups=mesh['dp'=8,'shard'=4] {'dp'}, use_global_device_ids=true, to_apply=%region_3.4 | all-reduce | flops 2304 | bytes 9216 | tf_op jit(solution)/shard_map/psum | solution.py:421
  384.8 0.6 slice.10
  385.4 0.0 copy-done.2
  385.4 0.0 copy-done.4
  385.4 0.0 copy-done.5
  385.4 0.6 copy.43
  386.0 0.6 copy.41
  386.6 0.6 copy.42
  387.2 44.3 %all-reduce.3.cloned.1.call-done = bf16[2,6,128,512]{3,2,1,0:T(8,128)(2,1)} async-done(((bf16[2,6,128,512]{3,2,1,0:T(8,128)(2,1)}), bf16[2,6,128,512]{3,2,1,0:T(8,128)(2,1)}) %all-reduce.3.cloned.1.call-update) | async-done | bytes 1572880 | tf_op jit(solution)/shard_map/psum | solution.py:420
  431.6 0.0 copy-done
  431.6 9.0 %fusion.6 = (bf16[2,6,128,512]{3,2,1,0:T(8,128)(2,1)}, f32[2,6,128,512]{3,2,1,0:T(8,128)}, f32[2,6,128,512]{3,2,1,0:T(8,128)}, f32[2,6,128,512]{3,2,1,0:T(8,128)}) fusion(f32[2,6,128,512]{3,2,1,0:T(8,128)S(1)} %copy-done, f32[2,6,128,512]{3,2,1,0:T(8,128)} %param.16, bf16[2,6,128,512]{3,2,1,0:T(8,128)(2,1)} %all-reduce.3.cloned.1.call-done, ...), kind=kLoop, calls=%fused_computation.16 | loop fusion | flops 12582912 | bytes 22020096 | tf_op jit(solution)/shard_map/convert_element_type | solution.py:432
  (4 shorter events, 0.0 us)
Async XLA Ops:
  7.2 4.7 %copy-start.1 = (f32[2,9,128]{2,0,1:T(2,128)S(1)}, f32[2,9,128]{2,0,1:T(2,128)}, u32[]{:S(2)}) copy-start(f32[2,9,128]{2,0,1:T(2,128)} %param.15) | copy-start | bytes 27652
  7.2 121.5 %all-gather.2.cloned.1.call-start = ((), (), s32[]{:S(2)}) async-start(), calls=%async_computation.2 | async-start | bytes 7864320 | tf_op jit(solution)/shard_map/all_gather | solution.py:411
  10.5 338.1 %reduce-scatter.5.cloned.1.call-start = ((), (), s32[]{:S(2)}) async-start(), calls=%async_computation.3 | async-start | bytes 7864320 | tf_op jit(solution)/shard_map/reduce_scatter | solution.py:418
  239.4 0.8 copy-start.3
  239.5 145.9 %copy-start.2 = (f32[2,9,128]{2,0,1:T(2,128)S(1)}, f32[2,9,128]{2,0,1:T(2,128)}, u32[]{:S(2)}) copy-start(f32[2,9,128]{2,0,1:T(2,128)} %param.15) | copy-start | bytes 27652
  239.5 145.9 %copy-start.4 = (f32[2,9,128]{2,0,1:T(2,128)S(1)}, f32[2,9,128]{2,0,1:T(2,128)}, u32[]{:S(2)}) copy-start(f32[2,9,128]{2,0,1:T(2,128)} %param.19) | copy-start | bytes 27652
  239.5 145.9 %copy-start.5 = (f32[2,9,128]{2,0,1:T(2,128)S(1)}, f32[2,9,128]{2,0,1:T(2,128)}, u32[]{:S(2)}) copy-start(f32[2,9,128]{2,0,1:T(2,128)} %param.18) | copy-start | bytes 27652
  239.5 192.1 %copy-start = (f32[2,6,128,512]{3,2,1,0:T(8,128)S(1)}, f32[2,6,128,512]{3,2,1,0:T(8,128)}, u32[]{:S(2)}) copy-start(f32[2,6,128,512]{3,2,1,0:T(8,128)} %param.14) | copy-start | bytes 9437188
  239.5 131.9 %reduce-scatter.7.cloned.1.call-start = ((), (), s32[]{:S(2)}) async-start(), calls=%async_computation.5 | async-start | bytes 163840
  241.3 190.2 %all-reduce.3.cloned.1.call-start = ((), (), s32[]{:S(2)}) async-start(), calls=%async_computation.4 | async-start | bytes 3145728 | tf_op jit(solution)/shard_map/psum | solution.py:420
Sparse Core Ops, SparseCore 0:
  10.6 118.0 all-gather.1
  239.7 108.9 reduce-scatter.4
  351.5 19.9 reduce-scatter.6
  374.6 56.9 all-reduce.2

commit v2 on v1

v2 whole, which is shorter than its diff:
```python
import functools
import math

import jax
import jax.numpy as jnp
from jax import lax
from jax.experimental import pallas as pl
from jax.experimental.pallas import tpu as pltpu
from jax.sharding import PartitionSpec as P

HEADS = 8
beta_first = 0.5
beta_second = 0.55
learn_rate = 0.05
vector_rate = 0.25
decay_rate = 0.01
adam_eps = 1e-08
adam_step = 3.0
norm_eps = 1e-05

LOG2E = 1.4426950408889634
LN2 = 0.6931471805599453
NEG = -1e30
f32 = jnp.float32
bf16 = jnp.bfloat16
PAIR = 128
RB = 256


def dot(left, right):
    return jnp.dot(left, right, preferred_element_type=f32)


def dot_nt(left, right):
    return lax.dot_general(left, right, (((1,), (1,)), ((), ())), preferred_element_type=f32)


def dot_tn(left, right):
    return lax.dot_general(left, right, (((0,), (0,)), ((), ())), preferred_element_type=f32)


def gelu_parts(value):
    size = jnp.abs(value) * (1.0 / math.sqrt(2.0))
    step = 1.0 / (1.0 + 0.3275911 * size)
    bell = jnp.exp2(value * value * (-0.5 * LOG2E))
    poly = step * (0.254829592 + step * (-0.284496736 + step * (1.421413741 + step * (-1.453152027 + step * 1.061405429))))
    tail = 0.5 * poly * bell
    below = jnp.where(value < 0.0, tail, 1.0 - tail)
    return value * below, below + value * bell * (1.0 / math.sqrt(2.0 * math.pi))


def normalize(value):
    center = jnp.mean(value, axis=-1, keepdims=True)
    centered = value - center
    spread = jnp.mean(centered * centered, axis=-1, keepdims=True)
    inverse = lax.rsqrt(spread + norm_eps)
    return centered * inverse, inverse


def norm_back(grad, normed, inverse, gain):
    scaled = grad * gain
    return inverse * (
        scaled
        - jnp.mean(scaled, axis=-1, keepdims=True)
        - normed * jnp.mean(scaled * normed, axis=-1, keepdims=True)
    )


def lane_masks(rows=1):
    lane = lax.broadcasted_iota(jnp.int32, (rows, PAIR), 1)
    low = jnp.where(lane < 64, 1.0, 0.0)
    return low.astype(bf16), (1.0 - low).astype(bf16)


class Refs:
    pass


def fill_bias(m, known):
    tokens = m.key_bias.shape[0]
    row = lax.broadcasted_iota(jnp.int32, (tokens, PAIR), 0)
    lane = lax.broadcasted_iota(jnp.int32, (tokens, PAIR), 1)
    m.key_bias[...] = jnp.where((lane == 0) & (row >= known), NEG, 0.0).astype(bf16)


def project(m, layer, xb):
    tokens = xb.shape[0]
    scale = LOG2E / 8.0

    def block(index, carry):
        rows = pl.ds(pl.multiple_of(index * 2 * RB, 2 * RB), 2 * RB)
        low = xb[rows, :]
        m.q[layer, rows, :] = ((dot(low, m.mat(layer, 0)) + m.vec(layer, 0)) * scale).astype(bf16)
        m.k[layer, rows, :] = dot(low, m.mat(layer, 1)).astype(bf16)
        m.v[layer, rows, :] = (dot(low, m.mat(layer, 2)) + m.vec(layer, 1)).astype(bf16)
        return carry

    lax.fori_loop(0, tokens // (2 * RB), block, 0)


def probs_copy(m, layer, pair, slot, out):
    here, there = m.probs.at[slot], m.probs_hbm.at[layer, pair]
    if out:
        return pltpu.make_async_copy(here, there, m.probs_sem.at[slot])
    return pltpu.make_async_copy(there, here, m.probs_sem.at[slot])


def attend(m, layer, known, hook=None):
    tokens, width = m.q.shape[1:]
    pairs = width // PAIR
    masks = lane_masks()
    lane = lax.broadcasted_iota(jnp.int32, (RB, PAIR), 1)
    ones_lane = jnp.where(lane == 0, 1.0, 0.0).astype(bf16)
    eye = lax.broadcasted_iota(jnp.int32, (RB, RB), 0) == lax.broadcasted_iota(jnp.int32, (RB, RB), 1)
    col = lax.broadcasted_iota(jnp.int32, (1, RB), 1)
    blocks = tokens // RB

    def one_pair(pair, carry):
        if hook is not None:
            hook(pair)
        slot = lax.rem(pair, 2)
        cols = pl.ds(pl.multiple_of(pair * PAIR, PAIR), PAIR)

        @pl.when(pair >= 2)
        def _():
            probs_copy(m, layer, pair - 2, slot, True).wait()

        keys = m.k[layer, :, cols]
        keys_wide = jnp.concatenate([keys, m.key_bias[...]], axis=1)
        values = m.v[layer, :, cols]
        mixed = []
        for head in range(2):
            for block in range(blocks):
                rows = slice(block * RB, (block + 1) * RB)
                query = m.q[layer, rows, cols] * masks[head]
                query_wide = jnp.concatenate([query, ones_lane], axis=1)
                parts = []
                for other in range(blocks):
                    keys_rows = slice(other * RB, (other + 1) * RB)
                    if other == block:
                        part = dot_nt(query, keys[keys_rows])
                        hidden = jnp.where(col + block * RB >= known, NEG, 0.0)
                        part = jnp.where(eye, part, part + hidden)
                    else:
                        part = dot_nt(query_wide, keys_wide[keys_rows])
                    parts.append(part)
                scores = jnp.concatenate(parts, axis=1)
                peak = jnp.max(scores, axis=1, keepdims=True)
                m.probs[slot, head, rows, :] = jnp.exp2(scores - peak).astype(bf16)
            values_wide = values * masks[head] + masks[1 - head]
            mixed.append(dot(m.probs[slot, head], values_wide))
        probs_copy(m, layer, pair, slot, True).start()
        low = lax.broadcasted_iota(jnp.int32, (tokens, PAIR), 1) < 64
        raw = jnp.where(low, mixed[0], mixed[1])
        total = pltpu.roll(jnp.where(low, mixed[1], mixed[0]), 64, 1)
        inverse = 1.0 / total
        m.inv_total[layer, :, cols] = inverse.astype(bf16)
        mean = raw * inverse
        high = mean.astype(bf16)
        m.o[layer, :, cols] = high
        m.o_low[layer, :, cols] = (mean - high.astype(f32)).astype(bf16)
        return carry

    lax.fori_loop(0, pairs, one_pair, 0)
    for pair in (pairs - 2, pairs - 1):
        probs_copy(m, layer, pair, pair % 2, True).wait()


def feed_forward(m, layer, x_of, y_to):
    tokens = m.q.shape[1]

    def block(index, carry):
        rows = pl.ds(pl.multiple_of(index * RB, RB), RB)
        branch = dot(m.o[layer, rows, :], m.mat(layer, 3)) + m.vec(layer, 2)
        normed, inverse = normalize(x_of(rows) + branch)
        m.n1[layer, rows, :] = normed.astype(bf16)
        m.inv[rows, 2 * layer : 2 * layer + 1] = inverse
        first = normed * m.vec(layer, 5) + m.vec(layer, 6)
        pre = dot(first.astype(bf16), m.mat(layer, 4)) + m.vec(layer, 3)
        hidden, slope = gelu_parts(pre)
        low = hidden.astype(bf16)
        m.r[layer, rows, :] = low
        m.slope[layer, rows, :] = slope.astype(bf16)
        feed = dot(low, m.mat(layer, 5)) + m.vec(layer, 4)
        normed, inverse = normalize(first + feed)
        m.n2[layer, rows, :] = normed.astype(bf16)
        m.inv[rows, 2 * layer + 1 : 2 * layer + 2] = inverse
        y_to(rows, normed * m.vec(layer, 7) + m.vec(layer, 8))
        return carry

    lax.fori_loop(0, tokens // RB, block, 0)


def column_sum(value):
    rows, width = value.shape
    return jnp.sum(value.reshape(rows // 8, 8, width), axis=0)


def rows_back(m, layer, hook=None, ready=None):
    tokens = m.q.shape[1]
    for row in range(8):
        m.sums[row] = jnp.zeros_like(m.sums[row])

    def block(index, carry):
        if hook is not None:
            hook(index)
        rows = pl.ds(pl.multiple_of(index * RB, RB), RB)
        grad = m.g[rows, :]
        normed = m.n2[layer, rows, :].astype(f32)
        m.sums[0] += column_sum(grad * normed)
        m.sums[1] += column_sum(grad)
        back = norm_back(grad, normed, m.inv[rows, 2 * layer + 1 : 2 * layer + 2], m.vec(layer, 7))
        m.sums[2] += column_sum(back)
        low = back.astype(bf16)
        m.n2[layer, rows, :] = low
        pre = dot_nt(low, m.mat(layer, 5)) * m.slope[layer, rows, :].astype(f32)
        m.sums[3] += column_sum(pre)
        low = pre.astype(bf16)
        m.du[rows, :] = low
        grad = back + dot_nt(low, m.mat(layer, 4))
        normed = m.n1[layer, rows, :].astype(f32)
        m.sums[4] += column_sum(grad * normed)
        m.sums[5] += column_sum(grad)
        back = norm_back(grad, normed, m.inv[rows, 2 * layer : 2 * layer + 1], m.vec(layer, 5))
        m.sums[6] += column_sum(back)
        m.g[rows, :] = back
        low = back.astype(bf16)
        m.n1[layer, rows, :] = low
        m.inv_total[layer, rows, :] = (dot_nt(low, m.mat(layer, 3)) * m.inv_total[layer, rows, :].astype(f32)).astype(bf16)
        first = normed * m.vec(layer, 5) + m.vec(layer, 6)
        m.slope[layer, rows, :] = first.astype(bf16)
        return carry

    lax.fori_loop(0, tokens // RB, block, 0)
    for row, place in ((0, 7), (1, 8), (2, 4), (3, 3), (4, 5), (5, 6), (6, 2)):
        m.grad_vec(layer, place, jnp.sum(m.sums[row], axis=0, keepdims=True))
    if ready is not None:
        ready()
    m.grad_mat(layer, 5, dot_tn(m.r[layer], m.n2[layer]))
    m.grad_mat(layer, 4, dot_tn(m.slope[layer], m.du[...]))
    m.grad_mat(layer, 3, dot_tn(m.o[layer], m.n1[layer]))


def attend_back(m, layer, hook=None):
    tokens, width = m.q.shape[1:]
    pairs = width // PAIR
    masks = lane_masks()
    blocks = tokens // RB

    def one_pair(pair, carry):
        if hook is not None:
            hook(pair)
        slot = lax.rem(pair, 2)
        cols = pl.ds(pl.multiple_of(pair * PAIR, PAIR), PAIR)
        probs_copy(m, layer, pair, slot, False).wait()

        @pl.when(pair + 1 < pairs)
        def _():
            probs_copy(m, layer, pair + 1, 1 - slot, False).start()

        grad = m.inv_total[layer, :, cols]
        turned = pltpu.roll(
            grad.astype(f32) * (m.o[layer, :, cols].astype(f32) + m.o_low[layer, :, cols].astype(f32)), 64, 1
        )
        turned_high = turned.astype(bf16)
        turned_low = (turned - turned_high.astype(f32)).astype(bf16)
        values = m.v[layer, :, cols]
        keys = m.k[layer, :, cols]
        query_turned = m.q[layer, :, cols].T
        grad_turned = grad.T
        grad_query, grad_keys, grad_values = [], [], []
        for head in range(2):
            part = slice(head * 64, (head + 1) * 64)
            wide = jnp.concatenate(
                [grad * masks[head] - turned_high * masks[1 - head], -turned_low * masks[1 - head]], axis=1
            )
            values_wide = jnp.concatenate(
                [values * masks[head] + masks[1 - head], jnp.broadcast_to(masks[1 - head], values.shape)], axis=1
            )
            grad_values.append(dot(grad_turned[part], m.probs[slot, head]))
            for block in range(blocks):
                rows = slice(block * RB, (block + 1) * RB)
                score = dot_nt(wide[rows], values_wide)
                m.probs[slot, head, rows, :] = (score * m.probs[slot, head, rows, :].astype(f32)).astype(bf16)
            grad_keys.append(dot(query_turned[part], m.probs[slot, head]))
            grad_query.append(dot(m.probs[slot, head], keys))
        low = lax.broadcasted_iota(jnp.int32, (tokens, PAIR), 1) < 64
        m.q[layer, :, cols] = (jnp.where(low, grad_query[0], grad_query[1]) * 0.125).astype(bf16)
        m.k[layer, :, cols] = (jnp.concatenate(grad_keys, axis=0) * LN2).astype(bf16).T
        m.v[layer, :, cols] = jnp.concatenate(grad_values, axis=0).astype(bf16).T
        return carry

    lax.fori_loop(0, pairs, one_pair, 0)


def project_back(m, layer, xb, ready=None):
    tokens = m.q.shape[1]
    ones = jnp.ones((8, tokens), bf16)
    m.grad_vec(layer, 0, dot(ones, m.q[layer])[0:1])
    m.grad_vec(layer, 1, dot(ones, m.v[layer])[0:1])
    m.grad_mat(layer, 0, dot_tn(xb[...], m.q[layer]))
    m.grad_mat(layer, 1, dot_tn(xb[...], m.k[layer]))
    m.grad_mat(layer, 2, dot_tn(xb[...], m.v[layer]))
    if ready is not None:
        ready()

    def block(index, carry):
        rows = pl.ds(pl.multiple_of(index * RB, RB), RB)
        m.g[rows, :] = (
            m.g[rows, :]
            + dot_nt(m.q[layer, rows, :], m.mat(layer, 0))
            + dot_nt(m.k[layer, rows, :], m.mat(layer, 1))
            + dot_nt(m.v[layer, rows, :], m.mat(layer, 2))
        )
        return carry

    lax.fori_loop(0, tokens // RB, block, 0)


def start_refs(q, k, v, o, o_low, inv_total, n1, n2, inv, r, slope, g, x1, du, sums, key_bias,
               probs, probs_sem, probs_hbm):
    m = Refs()
    m.q, m.k, m.v, m.o, m.o_low, m.inv_total = q, k, v, o, o_low, inv_total
    m.n1, m.n2, m.inv, m.r, m.slope, m.g, m.x1 = n1, n2, inv, r, slope, g, x1
    m.du, m.sums, m.key_bias = du, sums, key_bias
    m.probs, m.probs_sem, m.probs_hbm = probs, probs_sem, probs_hbm
    return m


def shared_scratch(layers, count, width):
    both = (layers, count, width)
    one = (count, width)
    return [
        pltpu.VMEM(both, bf16), pltpu.VMEM(both, bf16), pltpu.VMEM(both, bf16), pltpu.VMEM(both, bf16),
        pltpu.VMEM(both, bf16), pltpu.VMEM(both, bf16), pltpu.VMEM(both, bf16), pltpu.VMEM(both, bf16),
        pltpu.VMEM((count, 2 * layers), f32),
        pltpu.VMEM(both, bf16), pltpu.VMEM(both, bf16),
        pltpu.VMEM(one, f32), pltpu.VMEM(one, bf16),
        pltpu.VMEM(one, bf16),
        pltpu.VMEM((8, 8, width), f32),
        pltpu.VMEM((count, PAIR), bf16),
        pltpu.VMEM((2, 2, count, count), bf16),
        pltpu.SemaphoreType.DMA((2,)),
    ]


SHARED = 18


def plain_kernel(length_ref, class_ref, x_ref, cot_ref, w_ref, vec_ref, act_ref, dx_ref, mats_ref, vecs_ref, probs_hbm, *rest):
    m = start_refs(*rest[:SHARED], probs_hbm)
    out_sem = rest[SHARED]
    m.mat = lambda layer, place: w_ref[layer, place]
    m.vec = lambda layer, place: vec_ref[layer, place : place + 1, :]

    def grad_mat(layer, place, value):
        mats_ref[layer, place] = value.astype(bf16)

    def grad_vec(layer, place, value):
        vecs_ref[layer, place : place + 1, :] = value

    m.grad_mat, m.grad_vec = grad_mat, grad_vec
    length, klass = length_ref[0], class_ref[0]
    known = jnp.where(klass == 0, length, (length + 1) // 2)
    fill_bias(m, known)
    project(m, 0, x_ref)
    attend(m, 0, known)

    def keep_next(rows, value):
        m.g[rows, :] = value
        m.x1[rows, :] = value.astype(bf16)

    feed_forward(m, 0, lambda rows: x_ref[rows, :].astype(f32), keep_next)
    project(m, 1, m.x1)
    attend(m, 1, known)
    probs_copy(m, 1, 0, 0, False).start()

    def finish(rows, value):
        valid = lax.broadcasted_iota(jnp.int32, (RB, 1), 0) + rows.start < length
        act_ref[rows, :] = jnp.where(valid, value, 0.0).astype(bf16)
        m.g[rows, :] = jnp.where(valid, cot_ref[rows, :].astype(f32), 0.0)

    feed_forward(m, 1, lambda rows: m.g[rows, :], finish)
    for layer, xb in ((1, m.x1), (0, x_ref)):
        rows_back(m, layer)
        attend_back(m, layer)
        if layer:
            probs_copy(m, layer - 1, 0, 0, False).start()
        project_back(m, layer, xb)
    copy = pltpu.make_async_copy(m.g, dx_ref, out_sem)
    copy.start()
    copy.wait()


def plain_pass(lengths, classes, tokens, cotangent, mats, vecs):
    count, width = tokens.shape
    layers = mats.shape[0]
    vmem = pl.BlockSpec(memory_space=pltpu.VMEM)
    smem = pl.BlockSpec(memory_space=pltpu.SMEM)
    hbm = pl.BlockSpec(memory_space=pl.ANY)
    outs = pl.pallas_call(
        plain_kernel,
        out_shape=[
            jax.ShapeDtypeStruct((count, width), bf16),
            jax.ShapeDtypeStruct((count, width), f32),
            jax.ShapeDtypeStruct(mats.shape, bf16),
            jax.ShapeDtypeStruct((layers, 16, width), f32),
            jax.ShapeDtypeStruct((layers, width // PAIR, 2, count, count), bf16),
        ],
        in_specs=[smem, smem, vmem, vmem, vmem, vmem],
        out_specs=[vmem, hbm, vmem, vmem, hbm],
        scratch_shapes=shared_scratch(layers, count, width) + [pltpu.SemaphoreType.DMA],
        compiler_params=pltpu.CompilerParams(vmem_limit_bytes=67043328),
    )(lengths, classes, tokens, cotangent, mats, vecs)
    return outs[:4]


def adam_update(param, grad, first, second, rate):
    first_new = beta_first * first + (1.0 - beta_first) * grad
    second_new = beta_second * second + (1.0 - beta_second) * grad * grad
    first_hat = first_new / (1.0 - beta_first**adam_step)
    second_hat = second_new / (1.0 - beta_second**adam_step)
    param_new = param - rate * (first_hat / (jnp.sqrt(second_hat) + adam_eps) + decay_rate * param)
    return (param_new, first_new, second_new)


def plain_body(tokens, lengths, classes, cotangent, weights, vectors, first_weights, second_weights, first_vectors, second_vectors):
    mats = lax.all_gather(weights.astype(bf16), "shard", axis=2, tiled=True)
    vecs = lax.all_gather(vectors.astype(bf16), "shard", axis=2, tiled=True).astype(f32)
    vecs = jnp.pad(vecs, ((0, 0), (0, 16 - vecs.shape[1]), (0, 0)))
    activations, input_grad, grad_mats, grad_vecs = plain_pass(lengths, classes, tokens[0], cotangent[0], mats, vecs)
    grad_vecs = grad_vecs[:, : vectors.shape[1]]
    total_mats = lax.psum_scatter(grad_mats, "shard", scatter_dimension=2, tiled=True)
    total_vecs = lax.psum_scatter(grad_vecs.astype(bf16), "shard", scatter_dimension=2, tiled=True)
    total_mats = lax.psum(total_mats, "dp").astype(f32)
    total_vecs = lax.psum(total_vecs, "dp").astype(f32)
    new_weights, new_first_weights, new_second_weights = adam_update(
        weights, total_mats, first_weights, second_weights, learn_rate
    )
    new_vectors, new_first_vectors, new_second_vectors = adam_update(
        vectors, total_vecs, first_vectors, second_vectors, vector_rate
    )
    return (
        activations[None], input_grad[None], new_weights, new_weights.astype(bf16), new_first_weights, new_second_weights,
        new_vectors, new_first_vectors, new_second_vectors, total_vecs[:, 0],
    )


MESH = pl.DeviceIdType.MESH


def remote(src, dst, sems, place, device):
    return pltpu.make_async_remote_copy(
        src_ref=src, dst_ref=dst, send_sem=sems[0].at[place], recv_sem=sems[1].at[place], device_id=device, device_id_type=MESH
    )


class Spot:
    def __init__(self, planes, shards):
        self.planes, self.shards = planes, shards
        self.d, self.z = lax.axis_index("dp"), lax.axis_index("shard")
        self.c, self.t = lax.rem(self.d, 2), lax.div(self.d, 2)

    def plane(self, step):
        return lax.rem(self.t + step, self.planes)

    def shard(self, step):
        return lax.rem(self.z + step, self.shards)

    def sibling(self):
        return (self.t * 2 + 1 - self.c, self.z)


class Weights:
    def __init__(self, spot, w, layer, first, index, z_sems, p_sems, c_sems):
        self.spot, self.index = spot, index
        self.z_sems, self.p_sems, self.c_sems = z_sems, p_sems, c_sems
        self.view = w.at[layer, first : first + 3]

    def z_copy(self, step):
        s = self.spot
        piece = self.view.at[:, s.z, s.t, s.c]
        return remote(piece, piece, self.z_sems, (self.index, step - 1), (s.d, s.shard(step)))

    def p_copy(self, z_step, t_step):
        s = self.spot
        piece = self.view.at[:, s.shard(s.shards - z_step), s.t, s.c]
        place = (self.index, z_step - 1, t_step - 1)
        return remote(piece, piece, self.p_sems, place, (s.plane(t_step) * 2 + s.c, s.z))

    def c_copy(self, z_step):
        s = self.spot
        piece = self.view.at[:, s.shard(s.shards - z_step), :, s.c]
        return remote(piece, piece, self.c_sems, (self.index, z_step - 1), s.sibling())

    def steps(self):
        return range(1, self.spot.shards)

    def send_z(self):
        for step in self.steps():
            self.z_copy(step).start()

    def send_p(self):
        for step in self.steps():
            self.z_copy(step).wait_recv()
            for other in range(1, self.spot.planes):
                self.p_copy(step, other).start()

    def send_c(self):
        for step in self.steps():
            for other in range(1, self.spot.planes):
                self.p_copy(step, other).wait_recv()
            self.c_copy(step).start()

    def arrive(self):
        for step in self.steps():
            self.c_copy(step).wait_recv()

    def close(self):
        for step in self.steps():
            self.z_copy(step).wait_send()
            self.c_copy(step).wait_send()
            for other in range(1, self.spot.planes):
                self.p_copy(step, other).wait_send()


class Piece:
    def __init__(self, spot, grads, from_core, from_plane, mine, from_shard, total, index, c_sems, p_sems, z_sems, a_sems):
        self.spot, self.index = spot, index
        self.grads, self.from_core, self.from_plane = grads, from_core, from_plane
        self.mine, self.from_shard, self.total = mine, from_shard, total
        self.c_sems, self.p_sems, self.z_sems, self.a_sems = c_sems, p_sems, z_sems, a_sems

    def c_copy(self):
        s = self.spot
        return remote(self.grads.at[:, :, 1 - s.c], self.from_core, self.c_sems, (self.index,), s.sibling())

    def p_copy(self, step):
        s = self.spot
        other = s.plane(step)
        return remote(
            self.from_core.at[:, :, other], self.from_plane.at[step - 1], self.p_sems, (self.index, step - 1), (other * 2 + s.c, s.z)
        )

    def z_copy(self, step):
        s = self.spot
        other = s.shard(step)
        return remote(self.mine.at[:, other], self.from_shard.at[step - 1], self.z_sems, (self.index, step - 1), (s.d, other))

    def a_copy(self, step):
        s = self.spot
        part = self.total.at[:, s.c, s.t]
        other = lax.rem(s.d + step, 2 * s.planes)
        return remote(part, part, self.a_sems, (self.index, step - 1), (other, s.z))

    def send_c(self):
        self.c_copy().start()

    def send_p(self):
        s = self.spot
        self.c_copy().wait_recv()
        for mat in range(self.grads.shape[0]):
            own = self.grads[mat, :, s.c].astype(f32)
            self.from_core[mat] = (self.from_core[mat].astype(f32) + own).astype(bf16)
        for step in range(1, s.planes):
            self.p_copy(step).start()

    def send_z(self):
        s = self.spot
        for step in range(1, s.planes):
            self.p_copy(step).wait_recv()
        total = self.from_core[:, :, s.t].astype(f32)
        for step in range(1, s.planes):
            total = total + self.from_plane[step - 1].astype(f32)
        self.mine[...] = total.astype(bf16)
        for step in range(1, s.shards):
            self.z_copy(step).start()

    def send_a(self):
        s = self.spot
        for step in range(1, s.shards):
            self.z_copy(step).wait_recv()
        total = self.mine[:, s.z].astype(f32)
        for step in range(1, s.shards):
            total = total + self.from_shard[step - 1].astype(f32)
        self.total[:, s.c, s.t] = total.astype(bf16)
        for step in range(1, 2 * s.planes):
            self.a_copy(step).start()

    def arrive(self):
        for step in range(1, 2 * self.spot.planes):
            self.a_copy(step).wait_recv()

    def close(self):
        for step in range(1, self.spot.planes):
            self.p_copy(step).wait_send()
        for step in range(1, self.spot.shards):
            self.z_copy(step).wait_send()
        for step in range(1, 2 * self.spot.planes):
            self.a_copy(step).wait_send()


def full_kernel(planes, shards,
                length_ref, class_ref, x_hbm, cot_hbm, w_hbm, first_hbm, second_hbm, vec_in, first_vec, second_vec,
                act_hbm, dx_hbm, new_w, low_w, new_first, new_second, vec_out, first_out, second_out, query_out, probs_hbm,
                *rest):
    m = start_refs(*rest[:SHARED], probs_hbm)
    (x_ref, w, vec_own, vec_all, grads, grad_vecs, grads_vec,
     core_in, plane_in, mine, shard_in, total,
     core_in_v, plane_in_v, mine_v, shard_in_v, total_v,
     adam, adam_low,
     x_sem, stage_sem, load_sem, store_sem, out_sem,
     vz0, vz1, wz0, wz1, wp0, wp1, wc0, wc1,
     gc0, gc1, gp0, gp1, gz0, gz1, ga0, ga1) = rest[SHARED:]
    spot = Spot(planes, shards)
    tokens, width = x_ref.shape
    layers = w.shape[0]
    share = width // shards

    def mat(layer, place):
        return w[layer, place].reshape(width, width)

    m.mat = mat
    m.vec = lambda layer, place: vec_all[layer, place : place + 1, :]

    def grad_mat(layer, place, value):
        slot = 1 if place < 3 else 0
        grads[slot, place % 3] = value.astype(bf16).reshape(grads.shape[2:])

    def grad_vec(layer, place, value):
        grad_vecs[layer, place : place + 1, :] = value

    m.grad_mat, m.grad_vec = grad_mat, grad_vec

    groups = [
        Weights(spot, w, layer, first, layer * 2 + first // 3, (wz0, wz1), (wp0, wp1), (wc0, wc1))
        for layer in range(layers) for first in (0, 3)
    ]
    sems = ((gc0, gc1), (gp0, gp1), (gz0, gz1), (ga0, ga1))

    def piece(index, slot):
        return Piece(spot, grads.at[slot], core_in.at[index], plane_in.at[index], mine.at[index], shard_in.at[index],
                     total.at[index], index, *sems)

    feed1, proj1, feed0, proj0 = piece(0, 0), piece(1, 1), piece(2, 0), piece(3, 1)
    vecs = Piece(spot, grads_vec, core_in_v, plane_in_v, mine_v, shard_in_v, total_v, 4, *sems)

    x_copy = pltpu.make_async_copy(x_hbm, x_ref, x_sem.at[0])
    cot_copy = pltpu.make_async_copy(cot_hbm, m.du, x_sem.at[1])
    stages = [
        pltpu.make_async_copy(w_hbm.at[g // 2, 3 * (g % 2) : 3 * (g % 2) + 3], adam.at[g % 2, g // 2], stage_sem.at[g])
        for g in range(4)
    ]
    for copy in stages:
        copy.start()
    x_copy.start()
    cot_copy.start()

    barrier = pltpu.get_barrier_semaphore()
    for step in range(1, 2 * planes):
        pl.semaphore_signal(barrier, inc=1, device_id=(lax.rem(spot.d + step, 2 * planes), spot.z), device_id_type=MESH)
    for step in range(1, shards):
        pl.semaphore_signal(barrier, inc=1, device_id=(spot.d, spot.shard(step)), device_id_type=MESH)

    def cast(g):
        stages[g].wait()
        for place in range(3):
            low = adam[g % 2, g // 2, place].astype(bf16)
            w[g // 2, 3 * (g % 2) + place, spot.z] = low.reshape(w.shape[3:])

    cast(0)
    for layer in range(layers):
        vec_own[spot.z, layer] = jnp.zeros(vec_own.shape[2:], bf16)
        vec_own[spot.z, layer, 0 : vec_in.shape[1]] = vec_in[layer].astype(bf16)
    pl.semaphore_wait(barrier, 2 * planes - 1 + shards - 1)
    groups[0].send_z()

    def v_copy(step):
        part = vec_own.at[spot.z]
        return remote(part, part, (vz0, vz1), (step - 1,), (spot.d, spot.shard(step)))

    for step in range(1, shards):
        v_copy(step).start()
    for g in range(1, 4):
        cast(g)
    length, klass = length_ref[0], class_ref[0]
    known = jnp.where(klass == 0, length, (length + 1) // 2)
    fill_bias(m, known)
    grad_vecs[...] = jnp.zeros_like(grad_vecs)
    grads_vec[...] = jnp.zeros_like(grads_vec)

    def adam_loads(layer, first, slot):
        here = (slice(first, first + 3),)
        return [
            pltpu.make_async_copy(source.at[layer, first : first + 3], adam.at[slot, which], load_sem.at[slot, which])
            for which, source in enumerate((w_hbm, first_hbm, second_hbm))
        ]

    def adam_stores(layer, first, slot):
        copies = [
            pltpu.make_async_copy(adam.at[slot, which], target.at[layer, first : first + 3], store_sem.at[slot, which])
            for which, target in enumerate((new_w, new_first, new_second))
        ]
        copies.append(pltpu.make_async_copy(adam_low.at[slot], low_w.at[layer, first : first + 3], store_sem.at[slot, 3]))
        return copies

    def start(copies):
        for copy in copies:
            copy.start()

    def wait(copies):
        for copy in copies:
            copy.wait()

    def adam_step_of(layer, first, slot, part):
        wait(adam_loads(layer, first, slot))
        part.arrive()

        def one(place, carry):
            grad = part.total[place].reshape(share, width).astype(f32)
            param, one_moment, two_moment = adam_update(
                adam[slot, 0, place], grad, adam[slot, 1, place], adam[slot, 2, place], learn_rate
            )
            adam[slot, 0, place] = param
            adam[slot, 1, place] = one_moment
            adam[slot, 2, place] = two_moment
            adam_low[slot, place] = param.astype(bf16)
            return carry

        lax.fori_loop(0, 3, one, 0)
        start(adam_stores(layer, first, slot))

    groups[0].send_p()
    groups[1].send_z()
    groups[0].send_c()
    groups[1].send_p()
    groups[2].send_z()
    start(adam_loads(1, 3, 0))
    start(adam_loads(1, 0, 1))
    for step in range(1, shards):
        v_copy(step).wait_recv()
    for other in range(shards):
        vec_all[:, :, other * share : (other + 1) * share] = vec_own[other].astype(f32)
    x_copy.wait()
    groups[0].arrive()
    project(m, 0, x_ref)

    def on(index, value, action):
        pl.when(index == value)(action)

    def hook_forward(pair):
        def first():
            groups[1].send_c()
            groups[2].send_p()
            groups[3].send_z()

        def second():
            groups[2].send_c()
            groups[3].send_p()

        on(pair, 1, first)
        on(pair, 2, second)
        on(pair, 3, groups[3].send_c)

    attend(m, 0, known, hook_forward)

    def keep_next(rows, value):
        m.g[rows, :] = value
        m.x1[rows, :] = value.astype(bf16)

    groups[1].arrive()
    feed_forward(m, 0, lambda rows: x_ref[rows, :].astype(f32), keep_next)
    groups[2].arrive()
    project(m, 1, m.x1)
    attend(m, 1, known)
    probs_copy(m, 1, 0, 0, False).start()
    cot_copy.wait()

    def finish(rows, value):
        valid = lax.broadcasted_iota(jnp.int32, (RB, 1), 0) + rows.start < length
        m.probs[1, 0, rows, 0:width] = jnp.where(valid, value, 0.0).astype(bf16)
        m.g[rows, :] = jnp.where(valid, m.du[rows, :].astype(f32), 0.0)

    groups[3].arrive()
    feed_forward(m, 1, lambda rows: m.g[rows, :], finish)
    act_copy = pltpu.make_async_copy(m.probs.at[1, 0, :, 0:width], act_hbm, x_sem.at[2])
    act_copy.start()

    rows_back(m, 1)
    feed1.send_c()
    act_copy.wait()

    def hook_one(pair):
        on(pair, 1, feed1.send_p)
        on(pair, 2, feed1.send_z)
        on(pair, 3, feed1.send_a)

    attend_back(m, 1, hook_one)
    probs_copy(m, 0, 0, 0, False).start()
    project_back(m, 1, m.x1, proj1.send_c)
    adam_step_of(1, 3, 0, feed1)
    proj1.send_p()

    def hook_rows(index):
        on(index, 2, proj1.send_z)

    def ready():
        feed1.c_copy().wait_send()
        proj1.send_a()

    rows_back(m, 0, hook_rows, ready)
    feed0.send_c()

    def hook_two(pair):
        def first():
            adam_step_of(1, 0, 1, proj1)
            feed0.send_p()
            wait(adam_stores(1, 3, 0))
            start(adam_loads(0, 3, 0))

        def third():
            feed0.send_a()
            wait(adam_stores(1, 0, 1))
            start(adam_loads(0, 0, 1))

        on(pair, 1, first)
        on(pair, 2, feed0.send_z)
        on(pair, 3, third)

    attend_back(m, 0, hook_two)
    proj1.c_copy().wait_send()

    def ready_last():
        for layer in range(layers):
            for other in range(shards):
                part = grad_vecs[layer, :, other * share : (other + 1) * share]
                grads_vec[0, other, layer, 0] = part.astype(bf16)
        proj0.send_c()
        vecs.send_c()

    project_back(m, 0, x_ref, ready_last)
    dx_copy = pltpu.make_async_copy(m.g, dx_hbm, out_sem)
    dx_copy.start()
    proj0.send_p()
    vecs.send_p()
    adam_step_of(0, 3, 0, feed0)
    proj0.send_z()
    vecs.send_z()
    proj0.send_a()
    vecs.send_a()
    adam_step_of(0, 0, 1, proj0)
    vecs.arrive()
    count = vec_in.shape[1]
    for layer in range(layers):
        grad = total_v[0, layer, 0].astype(f32)[0:count]
        query_out[layer : layer + 1] = grad[0:1]
        param, one_moment, two_moment = adam_update(vec_in[layer], grad, first_vec[layer], second_vec[layer], vector_rate)
        vec_out[layer] = param
        first_out[layer] = one_moment
        second_out[layer] = two_moment
    for group in groups:
        group.close()
    for step in range(1, shards):
        v_copy(step).wait_send()
    feed0.c_copy().wait_send()
    proj0.c_copy().wait_send()
    vecs.c_copy().wait_send()
    for part in (feed1, proj1, feed0, proj0, vecs):
        part.close()
    wait(adam_stores(0, 3, 0))
    wait(adam_stores(0, 0, 1))
    dx_copy.wait()


def full_body(planes, shards, tokens, lengths, classes, cotangent, weights, vectors, first_weights, second_weights, first_vectors,
              second_vectors):
    _, count, width = tokens.shape
    layers = weights.shape[0]
    rows = width // (2 * planes * shards)
    share = width // shards
    vmem = pl.BlockSpec(memory_space=pltpu.VMEM)
    smem = pl.BlockSpec(memory_space=pltpu.SMEM)
    hbm = pl.BlockSpec(memory_space=pl.ANY)
    dma = pltpu.SemaphoreType.DMA

    def pieces(lead, mats, columns):
        return [
            pltpu.VMEM(lead + (mats, shards, planes, rows, columns), bf16),
            pltpu.VMEM(lead + (planes - 1, mats, shards, rows, columns), bf16),
            pltpu.VMEM(lead + (mats, shards, rows, columns), bf16),
            pltpu.VMEM(lead + (shards - 1, mats, rows, columns), bf16),
            pltpu.VMEM(lead + (mats, 2, planes, rows, columns), bf16),
        ]

    def twice(*shape):
        return [dma(shape), dma(shape)]

    scratch = shared_scratch(layers, count, width) + [
        pltpu.VMEM((count, width), bf16),
        pltpu.VMEM((layers, 6, shards, planes, 2, rows, width), bf16),
        pltpu.VMEM((shards, layers, 16, share), bf16),
        pltpu.VMEM((layers, 16, width), f32),
        pltpu.VMEM((2, 3, shards, 2, planes, rows, width), bf16),
        pltpu.VMEM((layers, 16, width), f32),
        pltpu.VMEM((1, shards, 2, planes, rows, share), bf16),
        *pieces((4,), 3, width),
        *pieces((), 1, share),
        pltpu.VMEM((2, 3, 3, share, width), f32),
        pltpu.VMEM((2, 3, share, width), bf16),
        dma((3,)), dma((4,)), dma((2, 3)), dma((2, 4)), dma,
        *twice(shards - 1),
        *twice(4, shards - 1), *twice(4, shards - 1, planes - 1), *twice(4, shards - 1),
        *twice(5), *twice(5, planes - 1), *twice(5, shards - 1), *twice(5, 2 * planes - 1),
    ]
    shape = jax.ShapeDtypeStruct
    outs = pl.pallas_call(
        functools.partial(full_kernel, planes, shards),
        out_shape=[
            shape((count, width), bf16), shape((count, width), f32),
            shape(weights.shape, f32), shape(weights.shape, bf16), shape(weights.shape, f32), shape(weights.shape, f32),
            shape(vectors.shape, f32), shape(vectors.shape, f32), shape(vectors.shape, f32), shape((layers, share), f32),
            shape((layers, width // PAIR, 2, count, count), bf16),
        ],
        in_specs=[smem, smem] + [hbm] * 5 + [vmem] * 3,
        out_specs=[hbm] * 6 + [vmem] * 4 + [hbm],
        scratch_shapes=scratch,
        compiler_params=pltpu.CompilerParams(vmem_limit_bytes=67043328, collective_id=0, has_side_effects=True),
    )(lengths, classes, tokens[0], cotangent[0], weights, first_weights, second_weights, vectors, first_vectors, second_vectors)
    return (outs[0][None], outs[1][None]) + tuple(outs[2:10])


def solution(mesh):
    devices, shards = mesh.shape["dp"], mesh.shape["shard"]

    def body(*args):
        width = args[0].shape[-1]
        layers = args[4].shape[0]
        rows, left = divmod(width, devices * shards)
        if devices % 2 == 0 and devices > 2 and shards > 1 and left == 0 and rows % 16 == 0 and layers == 2 and width // shards % PAIR == 0:
            return full_body(devices // 2, shards, *args)
        return plain_body(*args)

    cell = P(("dp", "shard"), None, None)
    mats = P(None, None, "shard", None)
    vecs = P(None, None, "shard")
    one = P(("dp", "shard"))
    in_specs = (cell, one, one, cell, mats, vecs, mats, mats, vecs, vecs)
    out_specs = (cell, cell, mats, mats, mats, mats, vecs, vecs, vecs, P(None, "shard"))
    return jax.shard_map(body, mesh=mesh, in_specs=in_specs, out_specs=out_specs, check_vma=False)
```

time: 447 us -> 208 us (0.47)
  waiting for transfers between devices: 277 us -> 0 us
  Pallas kernels: 111 us -> 185 us
  blocking collectives: 26.1 us -> 0 us
  local copies, waits for them, and re-layouts: 5.06 us -> 20.7 us
  between operations: 15.2 us -> 1.96 us
  other arithmetic: 12.9 us -> 0 us
    reduce_scatter x1 -> x0, waiting for transfers between devices: 107 us -> none  [body(): lax.psum_scatter(grad_mats, 'shard', scatter_dimension=2, tiled=True)]
    all_gather x1 -> x0, waiting for transfers between devices: 103 us -> none  [body(): mats = lax.all_gather(weights.astype(bf16), 'shard', axis=2, tiled=True)]
    pallas_call x1, Pallas kernels: 111 us -> 185 us  [full_body(): pl.pallas_call(functools.partial(full_kernel, planes, shards), out_shape=...]
    psum x1 -> x0, waiting for transfers between devices: 44.3 us -> none  [body(): total_mats = lax.psum(total_mats, 'dp').astype(f32)]
    unnamed x5 -> x0, waiting for transfers between devices: 22.8 us -> none
    unnamed x19 -> x25, local copies, waits for them, and re-layouts: 4.49 us -> 20.7 us
    all_gather x1 -> x0, blocking collectives: 13.6 us -> none  [body(): lax.all_gather(vectors.astype(bf16), 'shard', axis=2, tiled=True)]
    psum x1 -> x0, blocking collectives: 12.4 us -> none  [body(): total_vecs = lax.psum(total_vecs, 'dp').astype(f32)]
  transfers between devices with their start and end apart: 4 -> 0, of which waited for: 4 -> 0; matrix products, arithmetic and copies ran while one was open for 1% -> 0% of each run, Pallas kernels for 0% -> 0%
where the time goes in v2:
time: 208 us
  Pallas kernels  185 us (89%)
  local copies, waits for them, and re-layouts  20.7 us (10%)
    pallas_call x1, Pallas kernels, full_body(): pl.pallas_call(functools.partial(full_kernel, planes, shards), out_shape=...  185 us
    unnamed x25, local copies, waits for them, and re-layouts  20.7 us

profile of v2, /device:TPU:0, one launch (start us, length us, event | category | flops | bytes accessed | tf_op | source)
XLA Modules:
  0.0 207.5 jit_solution(14198478153043254200)
XLA Ops:
  1.9 1.3 copy.20.vec_in
  3.2 1.3 copy.21.first_vec
  4.5 1.3 copy.22.second_vec
  5.9 184.8 %shard_map.177 = (bf16[1024,512]{1,0:T(8,128)(2,1)}, f32[1024,512]{1,0:T(8,128)}, f32[2,6,128,512]{3,2,1,0:T(8,128)}, bf16[2,6,128,512]{3,2,1,0:T(8,128)(2,1)}, ...) custom-call(s32[1]{0:T(128)S(6)} %copy.33.length_ref, ...), custom_call_target="tpu_custom_call" | custom-call | tf_op jit(solution)/shard_map/pallas_call | solution.py:916
  190.7 0.0 copy-start.3
  190.7 1.5 copy.23
  192.2 1.3 copy.24
  193.5 1.3 copy.25
  194.8 0.0 copy-start.2
  194.8 2.4 %copy.35 = bf16[1,1024,512]{2,1,0:T(8,128)(2,1)} copy(bf16[1,1024,512]{2,1,0:T(8,128)(2,1)} %bitcast.7) | data formatting | bytes 2097152
  197.2 0.0 copy-done.3
  197.2 1.3 copy.36
  198.6 0.0 copy-done.2
  198.6 0.0 copy-start.4
  198.6 0.0 copy-start.1
  198.6 1.7 copy.37
  200.2 0.9 copy-done.4
  201.1 1.1 copy.38
  202.3 0.0 copy-done.1
  202.3 0.0 copy-start
  202.3 1.7 copy.39
  203.9 1.4 copy-done
  205.3 0.0 copy-start.5
  205.3 1.7 copy.40
  207.0 0.0 copy-done.5
  207.0 0.6 copy.41
Async XLA Ops:
  190.7 6.5 %copy-start.3 = (f32[1024,512]{1,0:T(8,128)S(1)}, f32[1024,512]{1,0:T(8,128)}, u32[]{:S(2)}) copy-start(f32[1024,512]{1,0:T(8,128)} %get-tuple-element.21) | copy-start | bytes 6291460
  194.8 3.7 %copy-start.2 = (f32[2,6,128,512]{3,2,1,0:T(8,128)S(1)}, f32[2,6,128,512]{3,2,1,0:T(8,128)}, u32[]{:S(2)}) copy-start(f32[2,6,128,512]{3,2,1,0:T(8,128)} %get-tuple-element.52) | copy-start | bytes 9437188
  198.6 2.5 %copy-start.4 = (bf16[2,6,128,512]{3,2,1,0:T(8,128)(2,1)S(1)}, bf16[2,6,128,512]{3,2,1,0:T(8,128)(2,1)}, u32[]{:S(2)}) copy-start(bf16[2,6,128,512]{3,2,1,0:T(8,128)(2,1)} %get-tuple-element.53) | copy-start | bytes 4718596
  198.6 3.7 %copy-start.1 = (f32[2,6,128,512]{3,2,1,0:T(8,128)S(1)}, f32[2,6,128,512]{3,2,1,0:T(8,128)}, u32[]{:S(2)}) copy-start(f32[2,6,128,512]{3,2,1,0:T(8,128)} %get-tuple-element.54) | copy-start | bytes 9437188
  202.3 3.0 %copy-start = (f32[2,6,128,512]{3,2,1,0:T(8,128)S(1)}, f32[2,6,128,512]{3,2,1,0:T(8,128)}, u32[]{:S(2)}) copy-start(f32[2,6,128,512]{3,2,1,0:T(8,128)} %get-tuple-element.55) | copy-start | bytes 9437188
  205.3 1.7 copy-start.5

commit v3 on v2

--- a/solution.py
+++ b/solution.py
@@ -81,6 +81,24 @@
     row = lax.broadcasted_iota(jnp.int32, (tokens, PAIR), 0)
     lane = lax.broadcasted_iota(jnp.int32, (tokens, PAIR), 1)
     m.key_bias[...] = jnp.where((lane == 0) & (row >= known), NEG, 0.0).astype(bf16)
+
+
+def project_one(m, layer, place, xb):
+    tokens = xb.shape[0]
+    scale = LOG2E / 8.0
+
+    def block(index, carry):
+        rows = pl.ds(pl.multiple_of(index * 2 * RB, 2 * RB), 2 * RB)
+        value = dot(xb[rows, :], m.mat(layer, place))
+        if place == 0:
+            m.q[layer, rows, :] = ((value + m.vec(layer, 0)) * scale).astype(bf16)
+        elif place == 1:
+            m.k[layer, rows, :] = value.astype(bf16)
+        else:
+            m.v[layer, rows, :] = (value + m.vec(layer, 1)).astype(bf16)
+        return carry
+
+    lax.fori_loop(0, tokens // (2 * RB), block, 0)
 
 
 def project(m, layer, xb):
@@ -241,15 +259,13 @@
     m.grad_mat(layer, 3, dot_tn(m.o[layer], m.n1[layer]))
 
 
-def attend_back(m, layer, hook=None):
+def attend_back(m, layer, hook=None, xb=None):
     tokens, width = m.q.shape[1:]
     pairs = width // PAIR
     masks = lane_masks()
     blocks = tokens // RB
 
     def one_pair(pair, carry):
-        if hook is not None:
-            hook(pair)
         slot = lax.rem(pair, 2)
         cols = pl.ds(pl.multiple_of(pair * PAIR, PAIR), PAIR)
         probs_copy(m, layer, pair, slot, False).wait()
@@ -284,27 +300,39 @@
                 m.probs[slot, head, rows, :] = (score * m.probs[slot, head, rows, :].astype(f32)).astype(bf16)
             grad_keys.append(dot(query_turned[part], m.probs[slot, head]))
             grad_query.append(dot(m.probs[slot, head], keys))
+            if hook is not None and head == 0:
+                hook(pair, 0)
         low = lax.broadcasted_iota(jnp.int32, (tokens, PAIR), 1) < 64
-        m.q[layer, :, cols] = (jnp.where(low, grad_query[0], grad_query[1]) * 0.125).astype(bf16)
-        m.k[layer, :, cols] = (jnp.concatenate(grad_keys, axis=0) * LN2).astype(bf16).T
-        m.v[layer, :, cols] = jnp.concatenate(grad_values, axis=0).astype(bf16).T
+        back_query = (jnp.where(low, grad_query[0], grad_query[1]) * 0.125).astype(bf16)
+        back_keys = (jnp.concatenate(grad_keys, axis=0) * LN2).astype(bf16)
+        back_values = jnp.concatenate(grad_values, axis=0).astype(bf16)
+        m.q[layer, :, cols] = back_query
+        m.k[layer, :, cols] = back_keys.T
+        m.v[layer, :, cols] = back_values.T
+        if xb is not None:
+            m.grad_pair(layer, pair, dot(jnp.concatenate([back_query.T, back_keys, back_values], axis=0), xb[...]))
+        if hook is not None:
+            hook(pair, 1)
         return carry
 
     lax.fori_loop(0, pairs, one_pair, 0)
 
 
-def project_back(m, layer, xb, ready=None):
+def project_back(m, layer, xb=None, ready=None, hook=None):
     tokens = m.q.shape[1]
     ones = jnp.ones((8, tokens), bf16)
     m.grad_vec(layer, 0, dot(ones, m.q[layer])[0:1])
     m.grad_vec(layer, 1, dot(ones, m.v[layer])[0:1])
-    m.grad_mat(layer, 0, dot_tn(xb[...], m.q[layer]))
-    m.grad_mat(layer, 1, dot_tn(xb[...], m.k[layer]))
-    m.grad_mat(layer, 2, dot_tn(xb[...], m.v[layer]))
+    if xb is not None:
+        m.grad_mat(layer, 0, dot_tn(xb[...], m.q[layer]))
+        m.grad_mat(layer, 1, dot_tn(xb[...], m.k[layer]))
+        m.grad_mat(layer, 2, dot_tn(xb[...], m.v[layer]))
     if ready is not None:
         ready()
 
     def block(index, carry):
+        if hook is not None:
+            hook(index)
         rows = pl.ds(pl.multiple_of(index * RB, RB), RB)
         m.g[rows, :] = (
             m.g[rows, :]
@@ -472,10 +500,10 @@
 
 
 class Weights:
-    def __init__(self, spot, w, layer, first, index, z_sems, p_sems, c_sems):
+    def __init__(self, spot, w, layer, first, count, index, z_sems, p_sems, c_sems):
         self.spot, self.index = spot, index
         self.z_sems, self.p_sems, self.c_sems = z_sems, p_sems, c_sems
-        self.view = w.at[layer, first : first + 3]
+        self.view = w.at[layer, first : first + count]
 
     def z_copy(self, step):
         s = self.spot
@@ -525,11 +553,11 @@
 
 
 class Piece:
-    def __init__(self, spot, grads, from_core, from_plane, mine, from_shard, total, index, c_sems, p_sems, z_sems, a_sems):
+    def __init__(self, spot, grads, from_core, from_plane, mine, from_shard, total, index, c_sems, p_sems, z_sems, a_sems, b_sems):
         self.spot, self.index = spot, index
         self.grads, self.from_core, self.from_plane = grads, from_core, from_plane
         self.mine, self.from_shard, self.total = mine, from_shard, total
-        self.c_sems, self.p_sems, self.z_sems, self.a_sems = c_sems, p_sems, z_sems, a_sems
+        self.c_sems, self.p_sems, self.z_sems, self.a_sems, self.b_sems = c_sems, p_sems, z_sems, a_sems, b_sems
 
     def c_copy(self):
         s = self.spot
@@ -550,15 +578,19 @@
     def a_copy(self, step):
         s = self.spot
         part = self.total.at[:, s.c, s.t]
-        other = lax.rem(s.d + step, 2 * s.planes)
-        return remote(part, part, self.a_sems, (self.index, step - 1), (other, s.z))
+        return remote(part, part, self.a_sems, (self.index, step - 1), (s.plane(step) * 2 + s.c, s.z))
+
+    def b_copy(self):
+        s = self.spot
+        part = self.total.at[:, s.c]
+        return remote(part, part, self.b_sems, (self.index,), s.sibling())
 
     def send_c(self):
         self.c_copy().start()
 
     def send_p(self):
         s = self.spot
-        self.c_copy().wait_recv()
+        self.c_copy().wait()
         for mat in range(self.grads.shape[0]):
             own = self.grads[mat, :, s.c].astype(f32)
             self.from_core[mat] = (self.from_core[mat].astype(f32) + own).astype(bf16)
@@ -584,34 +616,37 @@
         for step in range(1, s.shards):
             total = total + self.from_shard[step - 1].astype(f32)
         self.total[:, s.c, s.t] = total.astype(bf16)
-        for step in range(1, 2 * s.planes):
+        for step in range(1, s.planes):
             self.a_copy(step).start()
 
+    def send_b(self):
+        for step in range(1, self.spot.planes):
+            self.a_copy(step).wait_recv()
+        self.b_copy().start()
+
     def arrive(self):
-        for step in range(1, 2 * self.spot.planes):
-            self.a_copy(step).wait_recv()
+        self.b_copy().wait_recv()
 
     def close(self):
         for step in range(1, self.spot.planes):
             self.p_copy(step).wait_send()
+            self.a_copy(step).wait_send()
         for step in range(1, self.spot.shards):
             self.z_copy(step).wait_send()
-        for step in range(1, 2 * self.spot.planes):
-            self.a_copy(step).wait_send()
+        self.b_copy().wait_send()
 
 
 def full_kernel(planes, shards,
-                length_ref, class_ref, x_hbm, cot_hbm, w_hbm, first_hbm, second_hbm, vec_in, first_vec, second_vec,
-                act_hbm, dx_hbm, new_w, low_w, new_first, new_second, vec_out, first_out, second_out, query_out, probs_hbm,
-                *rest):
+                length_ref, class_ref, x_hbm, cot_hbm, w_hbm, vec_in, act_hbm, dx_hbm, tot_hbm, tot_vec, probs_hbm, *rest):
     m = start_refs(*rest[:SHARED], probs_hbm)
-    (x_ref, w, vec_own, vec_all, grads, grad_vecs, grads_vec,
+    (x_ref, w, vec_own, vec_all, grads, pair_grads, grad_vecs, grads_vec,
      core_in, plane_in, mine, shard_in, total,
+     core_in_p, plane_in_p, mine_p, shard_in_p, total_p,
      core_in_v, plane_in_v, mine_v, shard_in_v, total_v,
-     adam, adam_low,
-     x_sem, stage_sem, load_sem, store_sem, out_sem,
+     stage,
+     x_sem, stage_sem, feed_sem, pair_sem, vec_sem, out_sem,
      vz0, vz1, wz0, wz1, wp0, wp1, wc0, wc1,
-     gc0, gc1, gp0, gp1, gz0, gz1, ga0, ga1) = rest[SHARED:]
+     gc0, gc1, gp0, gp1, gz0, gz1, ga0, ga1, gb0, gb1) = rest[SHARED:]
     spot = Spot(planes, shards)
     tokens, width = x_ref.shape
     layers = w.shape[0]
@@ -624,31 +659,52 @@
     m.vec = lambda layer, place: vec_all[layer, place : place + 1, :]
 
     def grad_mat(layer, place, value):
-        slot = 1 if place < 3 else 0
-        grads[slot, place % 3] = value.astype(bf16).reshape(grads.shape[2:])
+        grads[place - 3] = value.astype(bf16).reshape(grads.shape[1:])
+
+    def grad_pair(layer, pair, value):
+        turned = value.astype(bf16).T
+        for place in range(3):
+            part = turned[:, place * PAIR : (place + 1) * PAIR]
+            pair_grads[pair, place] = part.reshape(pair_grads.shape[2:])
 
     def grad_vec(layer, place, value):
         grad_vecs[layer, place : place + 1, :] = value
 
-    m.grad_mat, m.grad_vec = grad_mat, grad_vec
+    m.grad_mat, m.grad_vec, m.grad_pair = grad_mat, grad_vec, grad_pair
 
     groups = [
-        Weights(spot, w, layer, first, layer * 2 + first // 3, (wz0, wz1), (wp0, wp1), (wc0, wc1))
-        for layer in range(layers) for first in (0, 3)
+        Weights(spot, w, layer, first, count, index, (wz0, wz1), (wp0, wp1), (wc0, wc1))
+        for index, (layer, first, count) in enumerate(((0, 0, 1), (0, 1, 1), (0, 2, 1), (0, 3, 3), (1, 0, 3), (1, 3, 3)))
     ]
-    sems = ((gc0, gc1), (gp0, gp1), (gz0, gz1), (ga0, ga1))
-
-    def piece(index, slot):
-        return Piece(spot, grads.at[slot], core_in.at[index], plane_in.at[index], mine.at[index], shard_in.at[index],
-                     total.at[index], index, *sems)
-
-    feed1, proj1, feed0, proj0 = piece(0, 0), piece(1, 1), piece(2, 0), piece(3, 1)
-    vecs = Piece(spot, grads_vec, core_in_v, plane_in_v, mine_v, shard_in_v, total_v, 4, *sems)
+    sems = ((gc0, gc1), (gp0, gp1), (gz0, gz1), (ga0, ga1), (gb0, gb1))
+
+    pairs = width // PAIR
+
+    def feed_piece(layer):
+        i = layers - 1 - layer
+        return Piece(spot, grads, core_in.at[i], plane_in.at[i], mine.at[i], shard_in.at[i], total.at[i], i, *sems)
+
+    def pair_piece(layer, pair):
+        i = (layers - 1 - layer) * pairs + pair
+        return Piece(spot, pair_grads.at[pair], core_in_p.at[i], plane_in_p.at[i], mine_p.at[i], shard_in_p.at[i],
+                     total_p.at[i], layers + i, *sems)
+
+    def feed_out(layer):
+        i = layers - 1 - layer
+        return pltpu.make_async_copy(total.at[i], tot_hbm.at[layer, 3:6], feed_sem.at[i])
+
+    def pair_out(layer, pair):
+        i = (layers - 1 - layer) * pairs + pair
+        cols = pl.ds(pl.multiple_of(pair * PAIR, PAIR), PAIR)
+        return pltpu.make_async_copy(total_p.at[i], tot_hbm.at[layer, 0:3, :, :, :, cols], pair_sem.at[i])
+
+    feed1, feed0 = feed_piece(1), feed_piece(0)
+    vecs = Piece(spot, grads_vec, core_in_v, plane_in_v, mine_v, shard_in_v, total_v, layers * (pairs + 1), *sems)
 
     x_copy = pltpu.make_async_copy(x_hbm, x_ref, x_sem.at[0])
     cot_copy = pltpu.make_async_copy(cot_hbm, m.du, x_sem.at[1])
     stages = [
-        pltpu.make_async_copy(w_hbm.at[g // 2, 3 * (g % 2) : 3 * (g % 2) + 3], adam.at[g % 2, g // 2], stage_sem.at[g])
+        pltpu.make_async_copy(w_hbm.at[g // 2, 3 * (g % 2) : 3 * (g % 2) + 3], stage.at[g], stage_sem.at[g])
         for g in range(4)
     ]
     for copy in stages:
@@ -665,15 +721,18 @@
     def cast(g):
         stages[g].wait()
         for place in range(3):
-            low = adam[g % 2, g // 2, place].astype(bf16)
+            low = stage[g, place].astype(bf16)
             w[g // 2, 3 * (g % 2) + place, spot.z] = low.reshape(w.shape[3:])
 
     cast(0)
+    vec_all[...] = jnp.zeros_like(vec_all)
     for layer in range(layers):
-        vec_own[spot.z, layer] = jnp.zeros(vec_own.shape[2:], bf16)
-        vec_own[spot.z, layer, 0 : vec_in.shape[1]] = vec_in[layer].astype(bf16)
+        for place in range(vec_in.shape[0]):
+            vec_all[layer, place : place + 1, 0:share] = vec_in[place, layer : layer + 1, :]
+        vec_own[spot.z, layer] = vec_all[layer, :, 0:share].astype(bf16)
     pl.semaphore_wait(barrier, 2 * planes - 1 + shards - 1)
-    groups[0].send_z()
+    for g in range(3):
+        groups[g].send_z()
 
     def v_copy(step):
         part = vec_own.at[spot.z]
@@ -689,78 +748,39 @@
     grad_vecs[...] = jnp.zeros_like(grad_vecs)
     grads_vec[...] = jnp.zeros_like(grads_vec)
 
-    def adam_loads(layer, first, slot):
-        here = (slice(first, first + 3),)
-        return [
-            pltpu.make_async_copy(source.at[layer, first : first + 3], adam.at[slot, which], load_sem.at[slot, which])
-            for which, source in enumerate((w_hbm, first_hbm, second_hbm))
-        ]
-
-    def adam_stores(layer, first, slot):
-        copies = [
-            pltpu.make_async_copy(adam.at[slot, which], target.at[layer, first : first + 3], store_sem.at[slot, which])
-            for which, target in enumerate((new_w, new_first, new_second))
-        ]
-        copies.append(pltpu.make_async_copy(adam_low.at[slot], low_w.at[layer, first : first + 3], store_sem.at[slot, 3]))
-        return copies
-
-    def start(copies):
-        for copy in copies:
-            copy.start()
-
-    def wait(copies):
-        for copy in copies:
-            copy.wait()
-
-    def adam_step_of(layer, first, slot, part):
-        wait(adam_loads(layer, first, slot))
-        part.arrive()
-
-        def one(place, carry):
-            grad = part.total[place].reshape(share, width).astype(f32)
-            param, one_moment, two_moment = adam_update(
-                adam[slot, 0, place], grad, adam[slot, 1, place], adam[slot, 2, place], learn_rate
-            )
-            adam[slot, 0, place] = param
-            adam[slot, 1, place] = one_moment
-            adam[slot, 2, place] = two_moment
-            adam_low[slot, place] = param.astype(bf16)
-            return carry
-
-        lax.fori_loop(0, 3, one, 0)
-        start(adam_stores(layer, first, slot))
-
     groups[0].send_p()
-    groups[1].send_z()
+    groups[1].send_p()
     groups[0].send_c()
-    groups[1].send_p()
-    groups[2].send_z()
-    start(adam_loads(1, 3, 0))
-    start(adam_loads(1, 0, 1))
+    groups[2].send_p()
+    groups[1].send_c()
+    groups[3].send_z()
+    groups[2].send_c()
     for step in range(1, shards):
         v_copy(step).wait_recv()
     for other in range(shards):
         vec_all[:, :, other * share : (other + 1) * share] = vec_own[other].astype(f32)
     x_copy.wait()
-    groups[0].arrive()
-    project(m, 0, x_ref)
+    for place in range(3):
+        groups[place].arrive()
+        project_one(m, 0, place, x_ref)
+    groups[3].send_p()
+    groups[4].send_z()
 
     def on(index, value, action):
         pl.when(index == value)(action)
 
     def hook_forward(pair):
         def first():
-            groups[1].send_c()
-            groups[2].send_p()
-            groups[3].send_z()
-
-        def second():
-            groups[2].send_c()
-            groups[3].send_p()
+            groups[3].send_c()
+            groups[4].send_p()
+
+        def third():
+            groups[4].send_c()
+            groups[5].send_p()
 
         on(pair, 1, first)
-        on(pair, 2, second)
-        on(pair, 3, groups[3].send_c)
+        on(pair, 2, groups[5].send_z)
+        on(pair, 3, third)
 
     attend(m, 0, known, hook_forward)
 
@@ -768,9 +788,10 @@
         m.g[rows, :] = value
         m.x1[rows, :] = value.astype(bf16)
 
-    groups[1].arrive()
+    groups[3].arrive()
     feed_forward(m, 0, lambda rows: x_ref[rows, :].astype(f32), keep_next)
-    groups[2].arrive()
+    groups[5].send_c()
+    groups[4].arrive()
     project(m, 1, m.x1)
     attend(m, 1, known)
     probs_copy(m, 1, 0, 0, False).start()
@@ -781,7 +802,7 @@
         m.probs[1, 0, rows, 0:width] = jnp.where(valid, value, 0.0).astype(bf16)
         m.g[rows, :] = jnp.where(valid, m.du[rows, :].astype(f32), 0.0)
 
-    groups[3].arrive()
+    groups[5].arrive()
     feed_forward(m, 1, lambda rows: m.g[rows, :], finish)
     act_copy = pltpu.make_async_copy(m.probs.at[1, 0, :, 0:width], act_hbm, x_sem.at[2])
     act_copy.start()
@@ -790,85 +811,105 @@
     feed1.send_c()
     act_copy.wait()
 
-    def hook_one(pair):
-        on(pair, 1, feed1.send_p)
-        on(pair, 2, feed1.send_z)
-        on(pair, 3, feed1.send_a)
-
-    attend_back(m, 1, hook_one)
+    def hook_of(layer, feed):
+        def hook(pair, place):
+            if place == 0:
+                on(pair, 0, feed.send_p)
+                on(pair, 3, feed.send_a)
+                pl.when(pair >= 1)(pair_piece(layer, pair - 1).send_p)
+                pl.when(pair >= 2)(pair_piece(layer, pair - 2).send_z)
+                pl.when(pair >= 3)(pair_piece(layer, pair - 3).send_a)
+                if layer == 0:
+                    on(pair, 0, feed1.send_b)
+            else:
+                pair_piece(layer, pair).send_c()
+                on(pair, 1, feed.send_z)
+                if layer == 0:
+                    pair_piece(1, pair).send_b()
+
+        return hook
+
+    last = pairs - 1
+    attend_back(m, 1, hook_of(1, feed1), m.x1)
     probs_copy(m, 0, 0, 0, False).start()
-    project_back(m, 1, m.x1, proj1.send_c)
-    adam_step_of(1, 3, 0, feed1)
-    proj1.send_p()
+
+    def hook_dx1(index):
+        def second():
+            pair_piece(1, last).send_p()
+            pair_piece(1, last - 1).send_z()
+            pair_piece(1, last - 2).send_a()
+
+        on(index, 2, second)
+
+    project_back(m, 1, hook=hook_dx1)
 
     def hook_rows(index):
-        on(index, 2, proj1.send_z)
-
-    def ready():
-        feed1.c_copy().wait_send()
-        proj1.send_a()
-
-    rows_back(m, 0, hook_rows, ready)
+        def first():
+            pair_piece(1, last).send_z()
+            pair_piece(1, last - 1).send_a()
+
+        on(index, 1, first)
+        on(index, 3, pair_piece(1, last).send_a)
+
+    rows_back(m, 0, hook_rows)
     feed0.send_c()
-
-    def hook_two(pair):
-        def first():
-            adam_step_of(1, 0, 1, proj1)
-            feed0.send_p()
-            wait(adam_stores(1, 3, 0))
-            start(adam_loads(0, 3, 0))
-
-        def third():
-            feed0.send_a()
-            wait(adam_stores(1, 0, 1))
-            start(adam_loads(0, 0, 1))
-
-        on(pair, 1, first)
-        on(pair, 2, feed0.send_z)
-        on(pair, 3, third)
-
-    attend_back(m, 0, hook_two)
-    proj1.c_copy().wait_send()
+    attend_back(m, 0, hook_of(0, feed0), x_ref)
 
     def ready_last():
         for layer in range(layers):
             for other in range(shards):
                 part = grad_vecs[layer, :, other * share : (other + 1) * share]
                 grads_vec[0, other, layer, 0] = part.astype(bf16)
-        proj0.send_c()
         vecs.send_c()
 
-    project_back(m, 0, x_ref, ready_last)
+    def hook_dx0(index):
+        def first():
+            vecs.send_p()
+            pair_piece(0, last - 1).send_z()
+            pair_piece(0, last - 2).send_a()
+            feed0.send_b()
+
+        def third():
+            pair_piece(0, last).send_z()
+            vecs.send_z()
+            pair_piece(0, last - 1).send_a()
+
+        on(index, 0, pair_piece(0, last).send_p)
+        on(index, 1, first)
+        on(index, 3, third)
+
+    project_back(m, 0, ready=ready_last, hook=hook_dx0)
     dx_copy = pltpu.make_async_copy(m.g, dx_hbm, out_sem)
     dx_copy.start()
-    proj0.send_p()
-    vecs.send_p()
-    adam_step_of(0, 3, 0, feed0)
-    proj0.send_z()
-    vecs.send_z()
-    proj0.send_a()
+    for pair in range(last):
+        pair_piece(0, pair).send_b()
+    pair_piece(0, last).send_a()
     vecs.send_a()
-    adam_step_of(0, 0, 1, proj0)
+    pair_piece(0, last).send_b()
+    vecs.send_b()
+    for layer, feed in ((1, feed1), (0, feed0)):
+        feed.arrive()
+        feed_out(layer).start()
+        for pair in range(pairs):
+            pair_piece(layer, pair).arrive()
+            pair_out(layer, pair).start()
     vecs.arrive()
-    count = vec_in.shape[1]
-    for layer in range(layers):
-        grad = total_v[0, layer, 0].astype(f32)[0:count]
-        query_out[layer : layer + 1] = grad[0:1]
-        param, one_moment, two_moment = adam_update(vec_in[layer], grad, first_vec[layer], second_vec[layer], vector_rate)
-        vec_out[layer] = param
-        first_out[layer] = one_moment
-        second_out[layer] = two_moment
+    vec_copy = pltpu.make_async_copy(total_v.at[0, :, 0], tot_vec, vec_sem)
+    vec_copy.start()
     for group in groups:
         group.close()
     for step in range(1, shards):
         v_copy(step).wait_send()
-    feed0.c_copy().wait_send()
-    proj0.c_copy().wait_send()
-    vecs.c_copy().wait_send()
-    for part in (feed1, proj1, feed0, proj0, vecs):
-        part.close()
-    wait(adam_stores(0, 3, 0))
-    wait(adam_stores(0, 0, 1))
+    for layer, feed in ((1, feed1), (0, feed0)):
+        feed.close()
+        for pair in range(pairs):
+            pair_piece(layer, pair).close()
+    vecs.close()
+    for layer in (1, 0):
+        feed_out(layer).wait()
+        for pair in range(pairs):
+            pair_out(layer, pair).wait()
+    vec_copy.wait()
     dx_copy.wait()
 
 
@@ -878,6 +919,8 @@
     layers = weights.shape[0]
     rows = width // (2 * planes * shards)
     share = width // shards
+    pairs = width // PAIR
+    sent = layers * (pairs + 1) + 1
     vmem = pl.BlockSpec(memory_space=pltpu.VMEM)
     smem = pl.BlockSpec(memory_space=pltpu.SMEM)
     hbm = pl.BlockSpec(memory_space=pl.ANY)
@@ -900,33 +943,43 @@
         pltpu.VMEM((layers, 6, shards, planes, 2, rows, width), bf16),
         pltpu.VMEM((shards, layers, 16, share), bf16),
         pltpu.VMEM((layers, 16, width), f32),
-        pltpu.VMEM((2, 3, shards, 2, planes, rows, width), bf16),
+        pltpu.VMEM((3, shards, 2, planes, rows, width), bf16),
+        pltpu.VMEM((pairs, 3, shards, 2, planes, rows, PAIR), bf16),
         pltpu.VMEM((layers, 16, width), f32),
         pltpu.VMEM((1, shards, 2, planes, rows, share), bf16),
-        *pieces((4,), 3, width),
+        *pieces((layers,), 3, width),
+        *pieces((layers * pairs,), 3, PAIR),
         *pieces((), 1, share),
-        pltpu.VMEM((2, 3, 3, share, width), f32),
-        pltpu.VMEM((2, 3, share, width), bf16),
-        dma((3,)), dma((4,)), dma((2, 3)), dma((2, 4)), dma,
+        pltpu.VMEM((4, 3, share, width), f32),
+        dma((3,)), dma((4,)), dma((layers,)), dma((layers * pairs,)), dma, dma,
         *twice(shards - 1),
-        *twice(4, shards - 1), *twice(4, shards - 1, planes - 1), *twice(4, shards - 1),
-        *twice(5), *twice(5, planes - 1), *twice(5, shards - 1), *twice(5, 2 * planes - 1),
+        *twice(6, shards - 1), *twice(6, shards - 1, planes - 1), *twice(6, shards - 1),
+        *twice(sent), *twice(sent, planes - 1), *twice(sent, shards - 1), *twice(sent, planes - 1), *twice(sent),
     ]
     shape = jax.ShapeDtypeStruct
     outs = pl.pallas_call(
         functools.partial(full_kernel, planes, shards),
         out_shape=[
-            shape((count, width), bf16), shape((count, width), f32),
-            shape(weights.shape, f32), shape(weights.shape, bf16), shape(weights.shape, f32), shape(weights.shape, f32),
-            shape(vectors.shape, f32), shape(vectors.shape, f32), shape(vectors.shape, f32), shape((layers, share), f32),
-            shape((layers, width // PAIR, 2, count, count), bf16),
+            shape((count, width), bf16), shape((count, width), f32), shape((layers, 6, 2, planes, rows, width), bf16),
+            shape((layers, rows, share), bf16), shape((layers, pairs, 2, count, count), bf16),
         ],
-        in_specs=[smem, smem] + [hbm] * 5 + [vmem] * 3,
-        out_specs=[hbm] * 6 + [vmem] * 4 + [hbm],
+        in_specs=[smem, smem] + [hbm] * 3 + [vmem],
+        out_specs=[hbm] * 5,
         scratch_shapes=scratch,
         compiler_params=pltpu.CompilerParams(vmem_limit_bytes=67043328, collective_id=0, has_side_effects=True),
-    )(lengths, classes, tokens[0], cotangent[0], weights, first_weights, second_weights, vectors, first_vectors, second_vectors)
-    return (outs[0][None], outs[1][None]) + tuple(outs[2:10])
+    )(lengths, classes, tokens[0], cotangent[0], weights, jnp.transpose(vectors, (1, 0, 2)))
+    total_mats = outs[2].reshape(weights.shape).astype(f32)
+    total_vecs = outs[3][:, : vectors.shape[1]].astype(f32)
+    new_weights, new_first_weights, new_second_weights = adam_update(
+        weights, total_mats, first_weights, second_weights, learn_rate
+    )
+    new_vectors, new_first_vectors, new_second_vectors = adam_update(
+        vectors, total_vecs, first_vectors, second_vectors, vector_rate
+    )
+    return (
+        outs[0][None], outs[1][None], new_weights, new_weights.astype(bf16), new_first_weights, new_second_weights,
+        new_vectors, new_first_vectors, new_second_vectors, total_vecs[:, 0],
+    )
 
 
 def solution(mesh):
@@ -936,7 +989,7 @@
         width = args[0].shape[-1]
         layers = args[4].shape[0]
         rows, left = divmod(width, devices * shards)
-        if devices % 2 == 0 and devices > 2 and shards > 1 and left == 0 and rows % 16 == 0 and layers == 2 and width // shards % PAIR == 0:
+        if devices % 2 == 0 and devices > 2 and shards > 1 and left == 0 and rows == 16 and layers == 2 and width // shards % PAIR == 0:
             return full_body(devices // 2, shards, *args)
         return plain_body(*args)
 

time: 208 us -> 181 us (0.87)
  Pallas kernels: 185 us -> 162 us
  local copies, waits for them, and re-layouts: 20.7 us -> 5.66 us
  other arithmetic: 0 us -> 11 us
    pallas_call x1, Pallas kernels: 185 us -> 162 us  [full_body(): pl.pallas_call(functools.partial(full_kernel, planes, shards), out_shape=...]
    unnamed x25 -> x9, local copies, waits for them, and re-layouts: 20.7 us -> 5.09 us
    convert_element_type x0 -> x2, other arithmetic: none -> 10.2 us  [the longest x1 9.51 us: full_body(): new_weights.astype(bf16)]
where the time goes in v3:
time: 181 us; the launch traced here: 180 us
  Pallas kernels  162 us (90%)
  other arithmetic  11 us (6%)
  local copies, waits for them, and re-layouts  5.66 us (3%)
  between operations  1.96 us (1%)
    pallas_call x1, Pallas kernels, full_body(): pl.pallas_call(functools.partial(full_kernel, planes, shards), out_shape=...  162 us
    convert_element_type x1, other arithmetic, full_body(): new_weights.astype(bf16)  9.51 us
    unnamed x9, local copies, waits for them, and re-layouts  5.09 us

profile of v3, /device:TPU:0, one launch (start us, length us, event | category | flops | bytes accessed | tf_op | source)
XLA Modules:
  0.0 180.3 jit_solution(15922157563852847728)
XLA Ops:
  1.9 161.7 %shard_map.177 = (bf16[1024,512]{1,0:T(8,128)(2,1)}, f32[1024,512]{1,0:T(8,128)}, bf16[2,6,2,4,16,512]{5,4,3,2,1,0:T(8,128)(2,1)}, bf16[2,16,128]{2,1,0:T(8,128)(2,1)}, bf16[2,4,2,1024,1024]{4,3,2,1,0:T(8,128)(2,1)}) custom-call(s32[1]{0:T(128)S(6)} %copy.46.length_ref, s32[1]{0:T(128)S(6)} %copy.47.class_ref, bf16[1024,512]{1,0:T(8,128)(2,1)} %bitcast.14, ...), custom_call_target="tpu_custom_call" | custom-call | tf_op jit(solution)/shard_map/pallas_call | solution.py:960
  163.7 0.7 slice_convert_fusion
  164.4 0.6 slice.8
  164.9 0.8 copy_subtract_fusion
  165.7 0.6 copy.24
  166.3 0.6 copy.26
  166.9 0.6 copy.25
  167.5 0.0 copy-start.1
  167.5 9.5 %fusion.7 = (bf16[2,6,128,512]{3,2,1,0:T(8,128)(2,1)}, f32[2,6,128,512]{3,2,1,0:T(8,128)}, f32[2,6,128,512]{3,2,1,0:T(8,128)}, f32[2,6,128,512]{3,2,1,0:T(8,128)}) fusion(f32[2,6,128,512]{3,2,1,0:T(8,128)} %w_hbm.1, f32[2,6,128,512]{3,2,1,0:T(8,128)} %param.16, bf16[2,6,2,4,16,512]{5,4,3,2,1,0:T(8,128)(2,1)} %get-tuple-element.16, f32[2,6,128,512]{3,2,1,0:T(8,128)} %param.17), kind=kLoop, calls=%fused_computation.16 | loop fusion | flops 12582912 | bytes 22020096 | tf_op jit(solution)/shard_map/convert_element_type | solution.py:980
  177.0 0.0 copy-start
  177.0 0.0 copy-done.1
  177.0 1.0 copy.48
  178.0 1.0 copy-done
  179.0 1.3 copy.49
Async XLA Ops:
  167.5 9.5 %copy-start.1 = (bf16[1024,512]{1,0:T(8,128)(2,1)S(1)}, bf16[1024,512]{1,0:T(8,128)(2,1)}, u32[]{:S(2)}) copy-start(bf16[1024,512]{1,0:T(8,128)(2,1)} %get-tuple-element.14) | copy-start | bytes 3145732
  177.0 2.0 %copy-start = (f32[1024,512]{1,0:T(8,128)S(1)}, f32[1024,512]{1,0:T(8,128)}, u32[]{:S(2)}) copy-start(f32[1024,512]{1,0:T(8,128)} %get-tuple-element.15) | copy-start | bytes 6291460

commit v4 on v3

--- a/solution.py
+++ b/solution.py
@@ -446,8 +446,8 @@
 def adam_update(param, grad, first, second, rate):
     first_new = beta_first * first + (1.0 - beta_first) * grad
     second_new = beta_second * second + (1.0 - beta_second) * grad * grad
-    first_hat = first_new / (1.0 - beta_first**adam_step)
-    second_hat = second_new / (1.0 - beta_second**adam_step)
+    first_hat = first_new * (1.0 / (1.0 - beta_first**adam_step))
+    second_hat = second_new * (1.0 / (1.0 - beta_second**adam_step))
     param_new = param - rate * (first_hat / (jnp.sqrt(second_hat) + adam_eps) + decay_rate * param)
     return (param_new, first_new, second_new)
 
@@ -815,15 +815,15 @@
         def hook(pair, place):
             if place == 0:
                 on(pair, 0, feed.send_p)
-                on(pair, 3, feed.send_a)
                 pl.when(pair >= 1)(pair_piece(layer, pair - 1).send_p)
+                on(pair, 2, feed.send_z)
                 pl.when(pair >= 2)(pair_piece(layer, pair - 2).send_z)
                 pl.when(pair >= 3)(pair_piece(layer, pair - 3).send_a)
                 if layer == 0:
                     on(pair, 0, feed1.send_b)
             else:
                 pair_piece(layer, pair).send_c()
-                on(pair, 1, feed.send_z)
+                on(pair, 3, feed.send_a)
                 if layer == 0:
                     pair_piece(1, pair).send_b()
 
@@ -867,7 +867,6 @@
             vecs.send_p()
             pair_piece(0, last - 1).send_z()
             pair_piece(0, last - 2).send_a()
-            feed0.send_b()
 
         def third():
             pair_piece(0, last).send_z()
@@ -881,10 +880,12 @@
     project_back(m, 0, ready=ready_last, hook=hook_dx0)
     dx_copy = pltpu.make_async_copy(m.g, dx_hbm, out_sem)
     dx_copy.start()
-    for pair in range(last):
-        pair_piece(0, pair).send_b()
+    feed0.send_b()
+    pair_piece(0, 0).send_b()
     pair_piece(0, last).send_a()
     vecs.send_a()
+    for pair in range(1, last):
+        pair_piece(0, pair).send_b()
     pair_piece(0, last).send_b()
     vecs.send_b()
     for layer, feed in ((1, feed1), (0, feed0)):
@@ -911,6 +912,121 @@
             pair_out(layer, pair).wait()
     vec_copy.wait()
     dx_copy.wait()
+
+
+CHUNKS = 6
+
+
+def last_kernel(act_in, dx_in, total_in, w_in, first_in, second_in, tot_vec, vec_ref, vec_first, vec_second,
+                act_out, dx_out, new_w, low_w, new_first, new_second, vec_out, first_out, second_out, query_out,
+                act, dx, total, w, first, second, low, token_load, token_store, loads, stores):
+    rows = w.shape[0] // CHUNKS
+
+    def piece(chunk):
+        return pl.ds(pl.multiple_of(chunk * rows, rows), rows)
+
+    def load(chunk):
+        part = piece(chunk)
+        return [
+            pltpu.make_async_copy(source.at[part], here.at[part], loads.at[which, chunk])
+            for which, (source, here) in enumerate(((w_in, w), (total_in, total), (first_in, first), (second_in, second)))
+        ]
+
+    def store(chunk):
+        part = piece(chunk)
+        return [
+            pltpu.make_async_copy(here.at[part], target.at[part], stores.at[which, chunk])
+            for which, (here, target) in enumerate(((w, new_w), (low, low_w), (first, new_first), (second, new_second)))
+        ]
+
+    ins = [pltpu.make_async_copy(dx_in, dx, token_load.at[0]), pltpu.make_async_copy(act_in, act, token_load.at[1])]
+    outs = [pltpu.make_async_copy(dx, dx_out, token_store.at[0]), pltpu.make_async_copy(act, act_out, token_store.at[1])]
+    for copy in load(0) + ins:
+        copy.start()
+    for chunk in range(1, CHUNKS):
+        for copy in load(chunk):
+            copy.start()
+
+    def one(chunk, carry):
+        for copy in load(chunk):
+            copy.wait()
+
+        def block(index, inner):
+            part = pl.ds(pl.multiple_of(chunk * rows + index * 16, 16), 16)
+            param, one_moment, two_moment = adam_update(
+                w[part, :], total[part, :].astype(f32), first[part, :], second[part, :], learn_rate
+            )
+            w[part, :] = param
+            low[part, :] = param.astype(bf16)
+            first[part, :] = one_moment
+            second[part, :] = two_moment
+            return inner
+
+        lax.fori_loop(0, rows // 16, block, 0)
+        for copy in store(chunk):
+            copy.start()
+        for which in range(2):
+
+            @pl.when(chunk == which)
+            def _():
+                ins[which].wait()
+                outs[which].start()
+
+        return carry
+
+    lax.fori_loop(0, CHUNKS, one, 0)
+    count, layers = vec_ref.shape[:2]
+    for layer in range(layers):
+        grads = tot_vec[layer].astype(f32)
+        for place in range(count):
+            one = slice(layer, layer + 1)
+            grad = grads[place : place + 1]
+            param, one_moment, two_moment = adam_update(
+                vec_ref[place, one, :], grad, vec_first[place, one, :], vec_second[place, one, :], vector_rate
+            )
+            vec_out[place, one, :] = param
+            first_out[place, one, :] = one_moment
+            second_out[place, one, :] = two_moment
+            if place == 0:
+                query_out[one, :] = grad
+    for copy in outs:
+        copy.wait()
+    for chunk in range(CHUNKS):
+        for copy in store(chunk):
+            copy.wait()
+
+
+def finish_step(parts, weights, vectors, first_weights, second_weights, first_vectors, second_vectors):
+    act, dx, total_mats, total_vecs = parts
+    count, width = act.shape
+    layers, places, share = vectors.shape
+    flat = lambda value: value.reshape(-1, width)
+    turned = lambda value: jnp.transpose(value, (1, 0, 2))
+    mat_rows = weights.size // width
+    hbm = pl.BlockSpec(memory_space=pl.ANY)
+    vmem = pl.BlockSpec(memory_space=pltpu.VMEM)
+    dma = pltpu.SemaphoreType.DMA
+    shape = jax.ShapeDtypeStruct
+    mat, low = (mat_rows, width), pltpu.VMEM((mat_rows, width), bf16)
+    outs = pl.pallas_call(
+        last_kernel,
+        out_shape=[
+            shape(act.shape, bf16), shape(dx.shape, f32), shape(mat, f32), shape(mat, bf16), shape(mat, f32), shape(mat, f32),
+            shape((places, layers, share), f32), shape((places, layers, share), f32), shape((places, layers, share), f32),
+            shape((layers, share), f32),
+        ],
+        in_specs=[hbm] * 6 + [vmem] * 4,
+        out_specs=[hbm] * 6 + [vmem] * 4,
+        scratch_shapes=[
+            pltpu.VMEM(act.shape, bf16), pltpu.VMEM(dx.shape, f32), low, pltpu.VMEM(mat, f32), pltpu.VMEM(mat, f32),
+            pltpu.VMEM(mat, f32), low, dma((2,)), dma((2,)), dma((4, CHUNKS)), dma((4, CHUNKS)),
+        ],
+        compiler_params=pltpu.CompilerParams(vmem_limit_bytes=67043328),
+    )(act, dx, flat(total_mats), flat(weights), flat(first_weights), flat(second_weights), total_vecs,
+      turned(vectors), turned(first_vectors), turned(second_vectors))
+    mats = [value.reshape(weights.shape) for value in outs[2:6]]
+    vecs = [turned(value) for value in outs[6:9]]
+    return (outs[0][None], outs[1][None], *mats, *vecs, outs[9])
 
 
 def full_body(planes, shards, tokens, lengths, classes, cotangent, weights, vectors, first_weights, second_weights, first_vectors,
@@ -968,18 +1084,7 @@
         scratch_shapes=scratch,
         compiler_params=pltpu.CompilerParams(vmem_limit_bytes=67043328, collective_id=0, has_side_effects=True),
     )(lengths, classes, tokens[0], cotangent[0], weights, jnp.transpose(vectors, (1, 0, 2)))
-    total_mats = outs[2].reshape(weights.shape).astype(f32)
-    total_vecs = outs[3][:, : vectors.shape[1]].astype(f32)
-    new_weights, new_first_weights, new_second_weights = adam_update(
-        weights, total_mats, first_weights, second_weights, learn_rate
-    )
-    new_vectors, new_first_vectors, new_second_vectors = adam_update(
-        vectors, total_vecs, first_vectors, second_vectors, vector_rate
-    )
-    return (
-        outs[0][None], outs[1][None], new_weights, new_weights.astype(bf16), new_first_weights, new_second_weights,
-        new_vectors, new_first_vectors, new_second_vectors, total_vecs[:, 0],
-    )
+    return finish_step(outs[:4], weights, vectors, first_weights, second_weights, first_vectors, second_vectors)
 
 
 def solution(mesh):

time: 181 us -> 174 us (0.961)
  other arithmetic: 11 us -> 0 us
  Pallas kernels: 162 us -> 172 us
  local copies, waits for them, and re-layouts: 5.66 us -> 0 us
    pallas_call x0 -> x1, Pallas kernels: none -> 11.7 us  [finish_step(): pl.pallas_call(last_kernel, out_shape=[shape(act.shape, bf16), shape(dx.s...]
    convert_element_type x2 -> x0, other arithmetic: 10.2 us -> none  [the longest x1 9.51 us: full_body(): new_weights.astype(bf16)]
    unnamed x9 -> x0, local copies, waits for them, and re-layouts: 5.09 us -> none
    pallas_call x1, Pallas kernels: 162 us -> 160 us  [full_body(): pl.pallas_call(functools.partial(full_kernel, planes, shards), out_shape=...]
where the time goes in v4:
time: 174 us
  Pallas kernels  172 us (99%)
  between operations  2.12 us (1%)
    pallas_call x1, Pallas kernels, full_body(): pl.pallas_call(functools.partial(full_kernel, planes, shards), out_shape=...  160 us
    pallas_call x1, Pallas kernels, finish_step(): pl.pallas_call(last_kernel, out_shape=[shape(act.shape, bf16), shape(dx.s...  11.7 us

profile of v4, /device:TPU:0, one launch (start us, length us, event | category | flops | bytes accessed | tf_op | source)
XLA Modules:
  0.0 173.7 jit_solution(14599266346066047799)
XLA Ops:
  1.9 159.9 %shard_map.177 = (bf16[1024,512]{1,0:T(8,128)(2,1)}, f32[1024,512]{1,0:T(8,128)}, bf16[2,6,2,4,16,512]{5,4,3,2,1,0:T(8,128)(2,1)}, bf16[2,16,128]{2,1,0:T(8,128)(2,1)}, bf16[2,4,2,1024,1024]{4,3,2,1,0:T(8,128)(2,1)}) custom-call(s32[1]{0:T(128)S(6)} %copy.20.length_ref, s32[1]{0:T(128)S(6)} %copy.21.class_ref, bf16[1024,512]{1,0:T(8,128)(2,1)} %bitcast.22, ...), custom_call_target="tpu_custom_call" | custom-call | tf_op jit(solution)/shard_map/pallas_call | solution.py:1076
  161.8 11.7 %shard_map.178 = (bf16[1024,512]{1,0:T(8,128)(2,1)}, f32[1024,512]{1,0:T(8,128)}, f32[1536,512]{1,0:T(8,128)}, bf16[1536,512]{1,0:T(8,128)(2,1)}, f32[1536,512]{...) custom-call(bf16[1024,512]{1,0:T(8,128)(2,1)} %get-tuple-element.24., ...), custom_call_target="tpu_custom_call" | custom-call | tf_op jit(solution)/shard_map/pallas_call | solution.py:1011

commit v5 on v4

--- a/solution.py
+++ b/solution.py
@@ -495,6 +495,16 @@
     def shard(self, step):
         return lax.rem(self.z + step, self.shards)
 
+    def partner(self, step):
+        if self.shards != 4:
+            return self.shard(self.shards - step)
+        odd, half = step % 2, step // 2
+        low, high = lax.rem(self.z, 2), lax.div(self.z, 2)
+        return low + odd - 2 * odd * low + 2 * (high + half - 2 * half * high)
+
+    def target(self, step):
+        return self.partner(step) if self.shards == 4 else self.shard(step)
+
     def sibling(self):
         return (self.t * 2 + 1 - self.c, self.z)
 
@@ -508,17 +518,17 @@
     def z_copy(self, step):
         s = self.spot
         piece = self.view.at[:, s.z, s.t, s.c]
-        return remote(piece, piece, self.z_sems, (self.index, step - 1), (s.d, s.shard(step)))
+        return remote(piece, piece, self.z_sems, (self.index, step - 1), (s.d, s.target(step)))
 
     def p_copy(self, z_step, t_step):
         s = self.spot
-        piece = self.view.at[:, s.shard(s.shards - z_step), s.t, s.c]
+        piece = self.view.at[:, s.partner(z_step), s.t, s.c]
         place = (self.index, z_step - 1, t_step - 1)
         return remote(piece, piece, self.p_sems, place, (s.plane(t_step) * 2 + s.c, s.z))
 
     def c_copy(self, z_step):
         s = self.spot
-        piece = self.view.at[:, s.shard(s.shards - z_step), :, s.c]
+        piece = self.view.at[:, s.partner(z_step), :, s.c]
         return remote(piece, piece, self.c_sems, (self.index, z_step - 1), s.sibling())
 
     def steps(self):
@@ -572,7 +582,7 @@
 
     def z_copy(self, step):
         s = self.spot
-        other = s.shard(step)
+        other = s.target(step)
         return remote(self.mine.at[:, other], self.from_shard.at[step - 1], self.z_sems, (self.index, step - 1), (s.d, other))
 
     def a_copy(self, step):
@@ -736,7 +746,7 @@
 
     def v_copy(step):
         part = vec_own.at[spot.z]
-        return remote(part, part, (vz0, vz1), (step - 1,), (spot.d, spot.shard(step)))
+        return remote(part, part, (vz0, vz1), (step - 1,), (spot.d, spot.target(step)))
 
     for step in range(1, shards):
         v_copy(step).start()

time: 174 us -> 174 us (level)
  no operation moved by 1% of the time
where the time goes in v5:
time: 174 us; the launch traced here: 173 us
  Pallas kernels  171 us (98%)
  between operations  2.12 us (1%)
    pallas_call x1, Pallas kernels, full_body(): pl.pallas_call(functools.partial(full_kernel, planes, shards), out_shape=...  160 us
    pallas_call x1, Pallas kernels, finish_step(): pl.pallas_call(last_kernel, out_shape=[shape(act.shape, bf16), shape(dx.s...  11.7 us

profile of v5, /device:TPU:0, one launch (start us, length us, event | category | flops | bytes accessed | tf_op | source)
XLA Modules:
  0.0 173.4 jit_solution(6274397459328760911)
XLA Ops:
  1.9 159.5 %shard_map.177 = (bf16[1024,512]{1,0:T(8,128)(2,1)}, f32[1024,512]{1,0:T(8,128)}, bf16[2,6,2,4,16,512]{5,4,3,2,1,0:T(8,128)(2,1)}, bf16[2,16,128]{2,1,0:T(8,128)(2,1)}, bf16[2,4,2,1024,1024]{4,3,2,1,0:T(8,128)(2,1)}) custom-call(s32[1]{0:T(128)S(6)} %copy.20.length_ref, s32[1]{0:T(128)S(6)} %copy.21.class_ref, bf16[1024,512]{1,0:T(8,128)(2,1)} %bitcast.22, ...), custom_call_target="tpu_custom_call" | custom-call | tf_op jit(solution)/shard_map/pallas_call | solution.py:1086
  161.5 11.7 %shard_map.178 = (bf16[1024,512]{1,0:T(8,128)(2,1)}, f32[1024,512]{1,0:T(8,128)}, f32[1536,512]{1,0:T(8,128)}, bf16[1536,512]{1,0:T(8,128)(2,1)}, f32[1536,512]{...) custom-call(bf16[1024,512]{1,0:T(8,128)(2,1)} %get-tuple-element.24., ...), custom_call_target="tpu_custom_call" | custom-call | tf_op jit(solution)/shard_map/pallas_call | solution.py:1021
